TPU v7x, 32 devices: a whole 2x2x4 slice. The times are simulated.
32 devices in a mesh: gx: 8 (over z, x), gy: 2 (over y), gz: 2 (over core).
Axes of the slice: x: 2, y: 2, z: 4, core: 2. Of those that a mesh axis runs over, the one named last changes fastest.
Arguments:
- patches: bfloat16 [8, 2, 3, 64, 64, 256], P(None, 'gy', None, 'gx', None, 'gz'), may hold values from -8 to 308
Outputs:
- smooth: float32 [3, 256, 64, 128], P(None, 'gx', 'gy', 'gz')
- confidence: float32 [256, 64, 128], P('gx', 'gy', 'gz')
All inputs are finite; a program needn't handle non-finite values.
Results may differ from a plain program's by a relative error of at most 0.0013.
Values may be sent and summed in bfloat16 or wider, within the bound.
No kernel may reach another device: no remote copies, remote signals or barrier semaphores. Data moves between devices by JAX's collectives and lax.ppermute only.
A program may use at most 192 MiB of HBM per device.

v0:
```python
import functools

import jax
import jax.numpy as jnp
import numpy as np
from jax import lax
from jax.experimental import pallas as pl
from jax.experimental.pallas import tpu as pltpu
from jax.sharding import PartitionSpec as P


KNEE = 0.5
BASE = 2.0**-5
POWER = 17
LOG2E = 1.4426950408889634


def encode(d):
    t = d * (BASE / KNEE) + jnp.where(d < 0.0, -BASE, BASE)
    p = t
    for _ in range(4):
        p = p * p
    return (p * t).astype(jnp.bfloat16)


def decode(code, scale=1.0):
    v = code.astype(jnp.float32)
    t = jnp.exp2(jnp.log(jnp.abs(v)) * (LOG2E / POWER))
    k = scale * (KNEE / BASE)
    return (t - BASE) * jnp.where(v < 0.0, -k, k)


def share(cell, length, paired):
    stride = length // 2
    centre, spread = (length - 1) / 2.0, length / 8.0
    other = jnp.where(cell < stride, cell + stride, cell - stride).astype(jnp.float32)
    mine = cell.astype(jnp.float32)
    ratio = ((mine - centre) ** 2 - (other - centre) ** 2) / (2.0 * spread * spread)
    alone = jnp.logical_and(cell < stride, jnp.logical_not(paired))
    return jnp.where(alone, 1.0, 1.0 / (1.0 + jnp.exp(ratio)))


def z_weights(length, depth):
    stride, count = length // 2, 2 * depth // (length // 2)
    u = np.arange(length, dtype=np.float64)
    g = np.exp(-((u - (length - 1) / 2.0) ** 2) / (2.0 * (length / 8.0) ** 2))
    table = np.zeros((count * length, 2 * depth), np.float32)
    for k in range(count):
        for w in range(length):
            z = k * stride + w
            if z < 2 * depth:
                alone = k == 0 and w < stride
                pair = 0.0 if alone else g[w + stride if w < stride else w - stride]
                table[k * length + w, z] = g[w] / (g[w] + pair)
    high = table.astype(jnp.bfloat16)
    low = (table - high.astype(np.float32)).astype(jnp.bfloat16)
    both = np.concatenate([high, low], 1)
    return np.stack([both, np.roll(both, count * length // 2, 0)])


def index(shape, axis):
    return lax.broadcasted_iota(jnp.int32, shape, axis)


def pick_kernel(dims, scal, patches, out, sem):
    count, half = dims["count"], dims["half"]
    start = dims["base"](scal[0], scal[2])
    rows = pl.ds((1 - scal[2]) * half, half)
    copy = pltpu.make_async_copy(patches.at[pl.ds(start, count), :, :, rows], out, sem)
    copy.start()
    copy.wait()


def fold_kernel(dims, scal, own_ref, recv_ref, w_ref, own_out, up_out, next_out, ny, edge):
    length, half, stride, first = dims["length"], dims["half"], dims["stride"], dims["first"]
    g, row, core = scal[0], scal[1], scal[2]
    begin = (g * 2 + core) * half
    upper = (begin >= stride).astype(jnp.int32)
    cell = index((length, 128), 0)
    ny[...] = share(cell, length, jnp.full(cell.shape, row) > 0)
    edge[...] = jnp.zeros_like(edge)
    shape = (8, 128)
    nx_pair = [
        share(jnp.full(shape, begin + u), length, jnp.full(shape, 1) > 0) for u in range(half)
    ]
    weights = w_ref[core]

    def body(i, carry):
        a = (g ^ (first + i)) - upper
        at = jnp.maximum(a, 0)
        recv_at = at - dims["base"](g, core)
        for u in range(half):
            nx = jnp.where(jnp.logical_and(a == 0, upper == 0), 1.0, nx_pair[u])
            nx = jnp.where(a < 0, 0.0, nx)
            both = (ny[...].reshape(-1, 8, 128) * nx).reshape(length, 128)
            rows = [
                jnp.concatenate([own_ref[at, 0, k, core * half + u], recv_ref[recv_at, 0, k, u]], 1)
                for k in range(3)
            ]
            part = jnp.dot(
                jnp.concatenate(rows, 0), weights, preferred_element_type=jnp.float32
            )
            part = part[:, :128] + part[:, 128:]
            for k in range(2):
                total = (part[(k + 1) * length : (k + 2) * length] - part[:length]) * both
                j = k * half + u
                own_out[i, j] = total[:stride]
                up_out[i, j * stride : (j + 1) * stride] = encode(total[stride:])
                for n, line in enumerate(dims["lines"]):
                    edge[2 * half * n + j : 2 * half * n + j + 1] = total[line : line + 1]
                next_out[i, j : j + 1] = total[stride : stride + 1]
        up_out[i, 2 * half * stride :] = encode(edge[...])
        return carry

    lax.fori_loop(0, dims["count"], body, 0, unroll=2)


def join_kernel(dims, scal, own_ref, next_ref, up_ref, down_ref, *refs):
    half, stride, count, edge_rows = dims["half"], dims["stride"], dims["count"], dims["edge"]
    far = refs[:-count]
    outs = refs[len(far) : len(far) + count]
    row, rows_y = scal[1], dims["rows_y"]
    from_below = (row > 0).astype(jnp.float32)
    from_above = (row < rows_y - 1).astype(jnp.float32)
    main, group = 2 * half * stride, 2 * half

    def body(j, carry):
        part = pl.ds(pl.multiple_of(j * stride, stride), stride)
        for k in range(count):
            outs[k][part] = encode(own_ref[k, j] + decode(up_ref[k, part], from_below))
        return carry

    lax.fori_loop(0, 2 * half, body, 0)
    for k in range(count):
        lo = decode(up_ref[k, main:], from_below)[:group]
        hi = next_ref[k] + decode(down_ref[k, main:], from_above)[group : 2 * group]
        for f in far:
            beyond = (row > 1).astype(jnp.float32)
            lo += decode(f[k, main:], beyond)[2 * group : 3 * group]
        both = jnp.concatenate([lo, hi], axis=0)
        if edge_rows > 2 * group:
            both = jnp.concatenate([both] * (edge_rows // (2 * group)), axis=0)
        outs[k][main:] = encode(both)


def z_sum(p):
    lanes = index(p.shape, p.ndim - 1)
    before = jnp.where(lanes == 0, 0.0, pltpu.roll(p, 1, p.ndim - 1))
    after = jnp.where(lanes == 127, 0.0, pltpu.roll(p, 127, p.ndim - 1))
    return before + p + after


def two_classes(d1, d2):
    top = jnp.maximum(jnp.maximum(d1, d2), 0.0)
    e0, e1, e2 = jnp.exp2(-top), jnp.exp2(d1 - top), jnp.exp2(d2 - top)
    inverse = 1.0 / (e0 + e1 + e2)
    return e0 * inverse, e1 * inverse


def ends_of(dims, scal, here, there, pad):
    half, stride = dims["half"], dims["stride"]
    main = slice(2 * half * stride, None)
    d = decode(here[main], LOG2E) + decode(there[main], LOG2E)
    row = scal[1]
    for k, p in enumerate(two_classes(d, jnp.concatenate([d[half:], d[:half]], axis=0))):
        for u in range(half):
            lo, hi = p[u : u + 1], p[2 * half + u : 2 * half + u + 1]
            pad[u, k, 7:8] = jnp.where(row > 0, lo, 0.0)
            pad[u, k, 8 + stride : 9 + stride] = jnp.where(row < dims["rows_y"] - 1, hi, 0.0)


def halves_of(dims, here, there, u, pad):
    half, stride = dims["half"], dims["stride"]

    def total(j):
        part = pl.ds(pl.multiple_of(j * stride, stride), stride)
        return decode(here[part], LOG2E) + decode(there[part], LOG2E)

    sums = []
    for k, p in enumerate(two_classes(total(u), total(half + u))):
        at = pad.at[u, k]
        at[8 : 8 + stride] = p
        sums.append(z_sum(at[7 : 7 + stride] + p + at[9 : 9 + stride]))
    left = index((stride, 128), 1) < 64
    return (
        jnp.where(left, sums[0], pltpu.roll(sums[1], 64, 1)),
        jnp.where(left, pltpu.roll(sums[0], 64, 1), sums[1]),
    )


def edge_kernel(dims, scal, *refs):
    half, slabs = dims["half"], dims["slabs"]
    codes, ends, pad = refs[: 2 * slabs], refs[-2], refs[-1]
    g, core = scal[0], scal[2]
    low = core == 0
    at = (g & (slabs - 1)) ^ jnp.where(low, 0, slabs - 1)
    u = jnp.where(low, 0, half - 1)
    for s in range(slabs):

        @pl.when(at == s)
        def _():
            ends_of(dims, scal, codes[s], codes[s + slabs], pad)
            z0, z1 = halves_of(dims, codes[s], codes[s + slabs], u, pad)
            ends[0] = z0
            ends[1] = z1


def smooth_kernel(dims, scal, *refs):
    half, slabs = dims["half"], dims["slabs"]
    codes, keep, send, pad = refs[: 2 * slabs], refs[-3], refs[-2], refs[-1]
    g, core = scal[0], scal[2]
    low = core == 0
    for s in range(slabs):
        t = (g & (slabs - 1)) ^ s
        mine = pad.at[s]
        ends_of(dims, scal, codes[s], codes[s + slabs], mine)
        for u in range(half):
            z0, z1 = halves_of(dims, codes[s], codes[s + slabs], u, mine)
            keep[t, u] = jnp.where(low, z0, z1)
            send[t, u] = jnp.where(low, z1, z0)


def finish_kernel(dims, scal, keep, recv, mine, theirs, smooth, confidence):
    half, stride, slabs, depth = dims["half"], dims["stride"], dims["slabs"], dims["depth"]
    step = dims["step"]
    g, row, core = scal[0], scal[1], scal[2]
    low = core == 0
    t = pl.program_id(0) * step

    def lower(at, u):
        return jnp.where(low, keep[at, u], recv[at, u])

    def higher(at, u):
        return jnp.where(low, recv[at, u], keep[at, u])

    first = jnp.where(low, theirs[core], mine[core])
    last = jnp.where(low, mine[core], theirs[core])
    lines = [jnp.where(t > 0, higher(jnp.maximum(t - 1, 0), half - 1), first)]
    for i in range(step):
        lines += [lower(t + i, u) for u in range(half)]
        lines += [higher(t + i, u) for u in range(half)]
    end = t + step
    lines += [jnp.where(end < slabs, lower(jnp.minimum(end, slabs - 1), 0), last)]
    shape = (stride, 128)
    y = row * stride + index(shape, 0)
    z = core * depth + (index(shape, 1) & (depth - 1))

    def line_count(cell, extent):
        return 3.0 - (cell == 0).astype(jnp.float32) - (cell == extent - 1).astype(jnp.float32)

    inverse = 1.0 / (line_count(y, dims["rows_y"] * stride) * line_count(z, 2 * depth))
    for i in range(2 * half * step):
        x = jnp.full((8, 128), g * stride + t * 2 * half + i)
        scale = 1.0 / line_count(x, dims["extent_x"])
        total = (lines[i] + lines[i + 1] + lines[i + 2]) * inverse
        total = (total.reshape(-1, 8, 128) * scale).reshape(shape)
        c0 = total[:, :depth]
        c1 = pltpu.roll(total, 64, 1)[:, :depth]
        c2 = jnp.maximum(1.0 - (c0 + c1), 0.0)
        smooth[0, i] = c0
        smooth[1, i] = c1
        smooth[2, i] = c2
        confidence[i] = jnp.maximum(jnp.maximum(c0, c1), c2)


def vmem(*shape):
    return pltpu.VMEM(shape, jnp.float32)


def whole(shape):
    return pl.BlockSpec(shape, lambda *_: (0,) * len(shape))


def like(shape, dtype=jnp.float32):
    return jax.ShapeDtypeStruct(shape, dtype)


def call(kernel, scal, args, outs, in_specs=None, out_specs=None, grid=(1,), scratch=(),
         mib=4, flops=0):
    args = list(args)
    size = sum(a.size * a.dtype.itemsize for a in args + list(outs))
    return pl.pallas_call(
        kernel,
        out_shape=list(outs),
        grid_spec=pltpu.PrefetchScalarGridSpec(
            num_scalar_prefetch=1,
            grid=grid,
            in_specs=in_specs or [whole(a.shape) for a in args],
            out_specs=out_specs or [whole(o.shape) for o in outs],
            scratch_shapes=list(scratch),
        ),
        compiler_params=pltpu.CompilerParams(vmem_limit_bytes=int(mib * 2**20)),
        cost_estimate=pl.CostEstimate(flops=flops, bytes_accessed=size, transcendentals=0),
    )(scal, *args)


def stitched(patches):
    positions, per_y, classes, slab, length, lanes = patches.shape
    nx_dev, ny_dev, nz_dev = (lax.axis_size(n) for n in ("gx", "gy", "gz"))
    stride = length // 2
    half = slab // nz_dev
    assert positions == nx_dev and per_y == 1 and classes == 3 and nz_dev == 2
    assert lanes == 128 and length == 64
    slabs = nx_dev // 2
    depth = lanes // 2
    far = int(ny_dev > 2)
    edge, edge_y = (-(-n * 2 * half // 16) * 16 for n in (2, 2 + far))
    main = 2 * half * stride
    rows, rows_up = main + edge, main + edge_y
    g, row, core = (lax.axis_index(n) for n in ("gx", "gy", "gz"))
    scal = jnp.stack([g, row, core]).astype(jnp.int32)
    dims = dict(
        length=length, half=half, stride=stride, slabs=slabs, rows=rows, edge=edge, far=far,
        rows_y=ny_dev, depth=depth, extent_x=positions * stride,
        lines=(stride - 1, 0) + (length - 1,) * far,
    )
    weights = jnp.asarray(z_weights(length, depth))

    def ship(array, axis, by):
        size = lax.axis_size(axis)
        pairs = [(i, i + by) for i in range(size) if 0 <= i + by < size]
        return lax.ppermute(array, axis, pairs)

    def upper(g, core):
        return ((g * 2 + core) * half >= stride).astype(jnp.int32)

    def swapped(first, mib):
        def base(g, core):
            start = ((g ^ first) & ~(slabs - 1)) - upper(g, core)
            return jnp.clip(start, 0, positions - slabs)

        (other,) = call(
            functools.partial(pick_kernel, dict(dims, count=slabs, base=base)), scal,
            [patches], [like((slabs, 1, 3, half, length, 128), jnp.bfloat16)],
            in_specs=[pl.BlockSpec(memory_space=pl.ANY)],
            scratch=[pltpu.SemaphoreType.DMA(())],
            mib=mib,
        )
        return lax.ppermute(other, "gz", [(0, 1), (1, 0)]), base

    def messages(first, count, recv, base):
        d = dict(dims, first=first, count=count, base=base)
        own, up, ahead = call(
            functools.partial(fold_kernel, d), scal, [patches, recv, weights],
            [
                like((count, 2 * half, stride, 128)),
                like((count, rows_up, 128), jnp.bfloat16),
                like((count, 2 * half, 128)),
            ],
            scratch=[vmem(length, 128), vmem(edge_y, 128)],
        )
        if ny_dev == 2:
            below = above = lax.ppermute(up, "gy", [(0, 1), (1, 0)])
        else:
            below, above = ship(up, "gy", 1), ship(up, "gy", -1)
        beyond = [ship(up, "gy", 2)] * far
        parts = call(
            functools.partial(join_kernel, d), scal,
            [own, ahead, below, above] + beyond,
            [like((rows, 128), jnp.bfloat16)] * count,
        )
        return [
            lax.ppermute(p, "gx", [(i, i ^ s) for i in range(nx_dev)]) if s else p
            for s, p in enumerate(parts, first)
        ]

    recv_far = swapped(slabs, 61.5)
    recv_near = swapped(0, 4)
    first = messages(slabs, slabs // 2, *recv_far)
    second = messages(slabs + slabs // 2, slabs // 2, *recv_far)
    third = messages(0, slabs, *recv_near)
    codes = third + first + second

    half_rows = (slabs, half, stride, 128)
    (ends,) = call(
        functools.partial(edge_kernel, dims), scal, codes, [like((2, stride, 128))],
        scratch=[vmem(half, 2, stride + 16, 128)],
    )
    above = [(2 * i + 1, 2 * i + 3) for i in range(nx_dev - 1)]
    below = [(2 * i + 2, 2 * i) for i in range(nx_dev - 1)]
    mine = lax.ppermute(ends, ("gx", "gz"), above + below)
    codes, _ = lax.optimization_barrier((codes, ends))
    keep, send = call(
        functools.partial(smooth_kernel, dims), scal, codes, [like(half_rows)] * 2,
        scratch=[vmem(slabs, half, 2, stride + 16, 128)],
    )
    recv = lax.ppermute(send, "gz", [(0, 1), (1, 0)])
    theirs = lax.ppermute(mine, "gz", [(0, 1), (1, 0)])

    step = slabs // 2
    return tuple(
        call(
            functools.partial(finish_kernel, dict(dims, step=step)), scal,
            [keep, recv, mine, theirs],
            [like((3, stride, stride, depth)), like((stride, stride, depth))],
            out_specs=[
                pl.BlockSpec((3, 2 * half * step, stride, depth), lambda i, s: (0, i, 0, 0)),
                pl.BlockSpec((2 * half * step, stride, depth), lambda i, s: (i, 0, 0)),
            ],
            grid=(slabs // step,),
            mib=8,
        )
    )


def solution(mesh):
    in_specs = (P(None, "gy", None, "gx", None, "gz"),)
    out_specs = (P(None, "gx", "gy", "gz"), P("gx", "gy", "gz"))
    return jax.shard_map(
        stitched, mesh=mesh, in_specs=in_specs, out_specs=out_specs, check_vma=False
    )
```

profile of v0, /device:TPU:0, one launch (start us, length us, event | category | flops | bytes accessed | tf_op | source)
XLA Modules:
  0.0 55.0 jit_solution(9461760173323041378)
XLA Ops:
  0.6 0.1 pad_add_fusion.scal
  0.7 1.9 %copy-done = bf16[8,1,3,8,64,128]{5,4,3,2,1,0:T(8,128)(2,1)S(1)} copy-done((bf16[8,1,3,8,64,128]{5,4,3,2,1,0:T(8,128)(2,1)S(1)}, bf16[8,1,3,8,64,128]{5,4,3,2,1,0:T(8,128)(2,1)}, u32[]{:S(2)}) %copy-start) | copy-done | bytes 3145752
  2.6 0.6 %shard_map.41 = bf16[4,1,3,4,64,128]{5,4,3,2,1,0:T(8,128)(2,1)S(1)} custom-call(s32[3]{0:T(128)S(1)} %pad_add_fusion.scal, bf16[8,1,3,8,64,128]{5,4,3,2,1,0:T(8,128)(2,1)S(1)} %copy-done), custom_call_target="tpu_custom_call" | custom-call | bytes 3932160 | tf_op jit(solution)/shard_map/pallas_call | solution.py:282
  3.2 0.6 %collective-permute-start = (bf16[4,1,3,4,64,128]{5,4,3,2,1,0:T(8,128)(2,1)S(1)}, bf16[4,1,3,4,64,128]{5,4,3,2,1,0:T(8,128)(2,1)S(1)}, u32[]{:S(2)}, u32[]{:S(2)}) collective-permute-start(bf16[4,1,3,4,64,128]{5,4,3,2,1,0:T(8,128)(2,1)S(1)} %shard_map.41), channel_id=1, source_target_pairs={{0,1},{1,0},{2,3},{3,2},{4,5},{5,4},{6,7},{7,6},{8,9},{9,8},{10,11... | collective-permute-start | bytes 2359304 | tf_op jit(solution)/shard_map/ppermute | solution.py:339
  3.8 0.0 copy-done.3
  3.8 2.7 %shard_map.44 = bf16[4,1,3,4,64,128]{5,4,3,2,1,0:T(8,128)(2,1)} custom-call(s32[3]{0:T(128)} %copy-done.3, bf16[8,1,3,8,64,128]{5,4,3,2,1,0:T(8,128)(2,1)} %own_ref.5), custom_call_target="tpu_custom_call" | custom-call | bytes 3932160 | tf_op jit(solution)/shard_map/pallas_call | solution.py:282
  6.5 0.1 collective-permute-start.5
  6.6 0.0 collective-permute-done.recv_ref
  6.6 0.0 copy-start.1
  6.6 1.9 %copy-done.1 = bf16[8,1,3,8,64,128]{5,4,3,2,1,0:T(8,128)(2,1)S(1)} copy-done((bf16[8,1,3,8,64,128]{5,4,3,2,1,0:T(8,128)(2,1)S(1)}, bf16[8,1,3,8,64,128]{5,4,3,2,1,0:T(8,128)(2,1)}, u32[]{:S(2)}) %copy-start.1) | copy-done | bytes 3145752
  8.5 0.7 %copy-done.4 = s32[3]{0:T(128)S(1)} copy-done((s32[3]{0:T(128)S(1)}, s32[3]{0:T(128)}, u32[]{:S(2)}) %copy-start.4) | copy-done | bytes 36
  9.1 1.4 %shard_map.42 = (f32[4,8,32,128]{3,2,1,0:T(8,128)S(1)}, bf16[4,272,128]{2,1,0:T(8,128)(2,1)S(1)}, f32[4,8,128]{2,1,0:T(8,128)S(1)}) custom-call(s32[3]{0:T(128)S(1)} %copy-done.4, bf16[8,1,3,8,64,128]{5,4,3,2,1,0:T(8,128)(2,1)S(1)} %copy-done.1, bf16[4,1,3,4,64,128]{5,4,3,2,1,0:T(8,128)(2,1)S(1)} %collective-permute-done.recv_ref, ...), custom_call_target="tpu_custom_call" | custom-call | bytes 5013504 | tf_op jit(solution)/shard_map/pallas_call | solution.py:282
  10.6 3.0 %collective-permute-start.1 = (bf16[4,272,128]{2,1,0:T(8,128)(2,1)S(1)}, bf16[4,272,128]{2,1,0:T(8,128)(2,1)S(1)}, u32[]{:S(2)}, u32[]{:S(2)}) collective-permute-start(bf16[4,272,128]{2,1,0:T(8,128)(2,1)S(1)} %get-tuple-element.31), channel_id=1, source_target_pairs={{0,2},{2,0},{1,3},{3,1},{4,6},{6,4},{5,7},{7,5},{8,10},{10,8},{9,1... | collective-permute-start | bytes 835592 | tf_op jit(solution)/shard_map/ppermute | solution.py:353
  13.6 0.0 collective-permute-done.5.recv_ref
  13.6 0.9 %shard_map.47 = (f32[2,8,32,128]{3,2,1,0:T(8,128)S(1)}, bf16[2,272,128]{2,1,0:T(8,128)(2,1)S(1)}, f32[2,8,128]{2,1,0:T(8,128)S(1)}) custom-call(s32[3]{0:T(128)S(1)} %copy-done.4, bf16[8,1,3,8,64,128]{5,4,3,2,1,0:T(8,128)(2,1)S(1)} %copy-done.1, bf16[4,1,3,4,64,128]{5,4,3,2,1,0:T(8,128)(2,1)S(1)} %collective-permute-done.5.recv_ref, ...), custom_call_target="tpu_custom_call" | custom-call | bytes 4603904 | tf_op jit(solution)/shard_map/pallas_call | solution.py:282
  14.6 0.0 copy-start.5
  14.6 0.1 collective-permute-start.9
  14.7 0.9 %shard_map.45 = (f32[2,8,32,128]{3,2,1,0:T(8,128)S(1)}, bf16[2,272,128]{2,1,0:T(8,128)(2,1)S(1)}, f32[2,8,128]{2,1,0:T(8,128)S(1)}) custom-call(s32[3]{0:T(128)S(1)} %copy-done.4, bf16[8,1,3,8,64,128]{5,4,3,2,1,0:T(8,128)(2,1)S(1)} %copy-done.1, bf16[4,1,3,4,64,128]{5,4,3,2,1,0:T(8,128)(2,1)S(1)} %collective-permute-done.5.recv_ref, ...), custom_call_target="tpu_custom_call" | custom-call | bytes 4603904 | tf_op jit(solution)/shard_map/pallas_call | solution.py:282
  15.6 2.1 %collective-permute-start.6 = (bf16[2,272,128]{2,1,0:T(8,128)(2,1)S(1)}, bf16[2,272,128]{2,1,0:T(8,128)(2,1)S(1)}, u32[]{:S(2)}, u32[]{:S(2)}) collective-permute-start(bf16[2,272,128]{2,1,0:T(8,128)(2,1)S(1)} %get-tuple-element.38), channel_id=1, source_target_pairs={{0,2},{2,0},{1,3},{3,1},{4,6},{6,4},{5,7},{7,5},{8,10},{10,8},{9,1... | collective-permute-start | bytes 417800 | tf_op jit(solution)/shard_map/ppermute | solution.py:353
  17.7 6.4 %collective-permute-done.9.up_ref.down_ref = bf16[2,272,128]{2,1,0:T(8,128)(2,1)S(1)} collective-permute-done((bf16[2,272,128]{2,1,0:T(8,128)(2,1)S(1)}, bf16[2,272,128]{2,1,0:T(8,128)(2,1)S(1)}, u32[]{:S(2)}, u32[]{:S(2)}) %collective-permute-start.9) | collective-permute-done | bytes 139296 | tf_op jit(solution)/shard_map/ppermute | solution.py:353
  24.1 0.9 %shard_map.48 = (bf16[272,128]{1,0:T(8,128)(2,1)S(1)}, bf16[272,128]{1,0:T(8,128)(2,1)S(1)}) custom-call(s32[3]{0:T(128)S(1)} %copy-done.4, f32[2,8,32,128]{3,2,1,0:T(8,128)S(1)} %get-tuple-element.41.own_ref, f32[2,8,128]{2,1,0:T(8,128)S(1)} %get-tuple-element.42.next_ref, bf16[2,272,128]{2,1,0:T(8,128)(2,1)S(1)} %collective-permute-done.9.up_ref.down_ref, ...), custom_call_target="tpu_custom_call" | custom-call | bytes 688128 | tf_op jit(solution)/shard_map/pallas_call | solution.py:282
  25.0 4.1 %collective-permute-start.10 = (bf16[272,128]{1,0:T(8,128)(2,1)S(1)}, bf16[272,128]{1,0:T(8,128)(2,1)S(1)}, u32[]{:S(2)}, u32[]{:S(2)}) collective-permute-start(bf16[272,128]{1,0:T(8,128)(2,1)S(1)} %get-tuple-element.44), channel_id=1, source_target_pairs={{0,24},{4,28},{8,16},{12,20},{16,8},{20,12},{24,0},{28,4},{1,25},{... | collective-permute-start | bytes 208904 | tf_op jit(solution)/shard_map/ppermute | solution.py:363
  29.1 1.2 %collective-permute-start.11 = (bf16[272,128]{1,0:T(8,128)(2,1)S(1)}, bf16[272,128]{1,0:T(8,128)(2,1)S(1)}, u32[]{:S(2)}, u32[]{:S(2)}) collective-permute-start(bf16[272,128]{1,0:T(8,128)(2,1)S(1)} %get-tuple-element.45), channel_id=1, source_target_pairs={{0,28},{4,24},{8,20},{12,16},{16,12},{20,8},{24,4},{28,0},{1,29},{... | collective-permute-start | bytes 208904 | tf_op jit(solution)/shard_map/ppermute | solution.py:363
  30.3 0.0 collective-permute-done.6.up_ref.down_ref
  30.3 0.9 %shard_map.46 = (bf16[272,128]{1,0:T(8,128)(2,1)S(1)}, bf16[272,128]{1,0:T(8,128)(2,1)S(1)}) custom-call(s32[3]{0:T(128)S(1)} %copy-done.4, f32[2,8,32,128]{3,2,1,0:T(8,128)S(1)} %get-tuple-element.36.own_ref, f32[2,8,128]{2,1,0:T(8,128)S(1)} %get-tuple-element.37.next_ref, bf16[2,272,128]{2,1,0:T(8,128)(2,1)S(1)} %collective-permute-done.6.up_ref.down_ref, ...), custom_call_target="tpu_custom_call" | custom-call | bytes 688128 | tf_op jit(solution)/shard_map/pallas_call | solution.py:282
  31.1 0.9 %collective-permute-start.7 = (bf16[272,128]{1,0:T(8,128)(2,1)S(1)}, bf16[272,128]{1,0:T(8,128)(2,1)S(1)}, u32[]{:S(2)}, u32[]{:S(2)}) collective-permute-start(bf16[272,128]{1,0:T(8,128)(2,1)S(1)} %get-tuple-element.39), channel_id=1, source_target_pairs={{0,16},{4,20},{8,24},{12,28},{16,0},{20,4},{24,8},{28,12},{1,17},{... | collective-permute-start | bytes 208904 | tf_op jit(solution)/shard_map/ppermute | solution.py:363
  32.0 2.0 %collective-permute-start.8 = (bf16[272,128]{1,0:T(8,128)(2,1)S(1)}, bf16[272,128]{1,0:T(8,128)(2,1)S(1)}, u32[]{:S(2)}, u32[]{:S(2)}) collective-permute-start(bf16[272,128]{1,0:T(8,128)(2,1)S(1)} %get-tuple-element.40), channel_id=1, source_target_pairs={{0,20},{4,16},{8,28},{12,24},{16,4},{20,0},{24,12},{28,8},{1,21},{... | collective-permute-start | bytes 208904 | tf_op jit(solution)/shard_map/ppermute | solution.py:363
  34.0 0.0 collective-permute-done.1.up_ref.down_ref
  34.0 1.1 %shard_map.43 = (bf16[272,128]{1,0:T(8,128)(2,1)S(1)}, bf16[272,128]{1,0:T(8,128)(2,1)S(1)}, bf16[272,128]{1,0:T(8,128)(2,1)S(1)}, bf16[272,128]{1,0:T(8,128)(2,1)S(1)}) custom-call(s32[3]{0:T(128)S(1)} %copy-done.4, f32[4,8,32,128]{3,2,1,0:T(8,128)S(1)} %get-tuple-element.29.own_ref, f32[4,8,128]{2,1,0:T(8,128)S(1)} %get-tuple-element.30.next_ref, ...), custom_call_target="tpu_custom_call" | custom-call | bytes 1376256 | tf_op jit(solution)/shard_map/pallas_call | solution.py:282
  35.0 1.7 %collective-permute-start.2 = (bf16[272,128]{1,0:T(8,128)(2,1)S(1)}, bf16[272,128]{1,0:T(8,128)(2,1)S(1)}, u32[]{:S(2)}, u32[]{:S(2)}) collective-permute-start(bf16[272,128]{1,0:T(8,128)(2,1)S(1)} %get-tuple-element.33), channel_id=1, source_target_pairs={{0,4},{4,0},{8,12},{12,8},{16,20},{20,16},{24,28},{28,24},{1,5},{5... | collective-permute-start | bytes 208904 | tf_op jit(solution)/shard_map/ppermute | solution.py:363
  36.7 0.0 collective-permute-done.10.refs_6_
  36.7 1.3 %collective-permute-start.3 = (bf16[272,128]{1,0:T(8,128)(2,1)S(1)}, bf16[272,128]{1,0:T(8,128)(2,1)S(1)}, u32[]{:S(2)}, u32[]{:S(2)}) collective-permute-start(bf16[272,128]{1,0:T(8,128)(2,1)S(1)} %get-tuple-element.34), channel_id=1, source_target_pairs={{0,8},{4,12},{8,0},{12,4},{16,24},{20,28},{24,16},{28,20},{1,9},{5... | collective-permute-start | bytes 208904 | tf_op jit(solution)/shard_map/ppermute | solution.py:363
  38.0 0.0 collective-permute-done.11.refs_7_
  38.0 0.5 collective-permute-start.4
  38.6 0.6 %collective-permute-done.7.refs_4_ = bf16[272,128]{1,0:T(8,128)(2,1)S(1)} collective-permute-done((bf16[272,128]{1,0:T(8,128)(2,1)S(1)}, bf16[272,128]{1,0:T(8,128)(2,1)S(1)}, u32[]{:S(2)}, u32[]{:S(2)}) %collective-permute-start.7) | collective-permute-done | bytes 69664 | tf_op jit(solution)/shard_map/ppermute | solution.py:363
  39.2 0.9 %collective-permute-done.8.refs_5_ = bf16[272,128]{1,0:T(8,128)(2,1)S(1)} collective-permute-done((bf16[272,128]{1,0:T(8,128)(2,1)S(1)}, bf16[272,128]{1,0:T(8,128)(2,1)S(1)}, u32[]{:S(2)}, u32[]{:S(2)}) %collective-permute-start.8) | collective-permute-done | bytes 69664 | tf_op jit(solution)/shard_map/ppermute | solution.py:363
  40.1 0.8 %collective-permute-done.2.refs_1_ = bf16[272,128]{1,0:T(8,128)(2,1)S(1)} collective-permute-done((bf16[272,128]{1,0:T(8,128)(2,1)S(1)}, bf16[272,128]{1,0:T(8,128)(2,1)S(1)}, u32[]{:S(2)}, u32[]{:S(2)}) %collective-permute-start.2) | collective-permute-done | bytes 69664 | tf_op jit(solution)/shard_map/ppermute | solution.py:363
  41.0 0.3 collective-permute-done.3.refs_2_
  41.3 2.0 %collective-permute-done.4.refs_3_ = bf16[272,128]{1,0:T(8,128)(2,1)S(1)} collective-permute-done((bf16[272,128]{1,0:T(8,128)(2,1)S(1)}, bf16[272,128]{1,0:T(8,128)(2,1)S(1)}, u32[]{:S(2)}, u32[]{:S(2)}) %collective-permute-start.4) | collective-permute-done | bytes 69664 | tf_op jit(solution)/shard_map/ppermute | solution.py:363
  43.3 0.8 %shard_map.49 = f32[2,32,128]{2,1,0:T(8,128)S(1)} custom-call(s32[3]{0:T(128)S(1)} %copy-done.4, bf16[272,128]{1,0:T(8,128)(2,1)S(1)} %get-tuple-element.46.refs_0_, bf16[272,128]{1,0:T(8,128)(2,1)S(1)} %collective-permute-done.2.refs_1_, bf16[272,128]{1,0:T(8,128)(2,1)S(1)} %collective-permute-done.3.refs_2_, ...), custom_call_target="tpu_custom_call" | custom-call | bytes 589824 | tf_op jit(solution)/shard_map/pallas_call | solution.py:282
  44.0 1.8 %shard_map.50 = (f32[4,4,32,128]{3,2,1,0:T(8,128)S(1)}, f32[4,4,32,128]{3,2,1,0:T(8,128)S(1)}) custom-call(s32[3]{0:T(128)S(1)} %copy-done.4, bf16[272,128]{1,0:T(8,128)(2,1)S(1)} %get-tuple-element.46.refs_0_, bf16[272,128]{1,0:T(8,128)(2,1)S(1)} %collective-permute-done.2.refs_1_, bf16[272,128]{1,0:T(8,128)(2,1)S(1)} %collective-permute-done.3.refs_2_, ...), custom_call_target="tpu_custom_call" | custom-call | bytes 1081344 | tf_op jit(solution)/shard_map/pallas_call | solution.py:282
  45.9 0.1 collective-permute-start.12
  45.9 1.3 %collective-permute-start.13 = (f32[2,32,128]{2,1,0:T(8,128)S(1)}, f32[2,32,128]{2,1,0:T(8,128)S(1)}, u32[]{:S(2)}, u32[]{:S(2)}) collective-permute-start(f32[2,32,128]{2,1,0:T(8,128)S(1)} %shard_map.49), channel_id=1, source_target_pairs={{1,5},{5,9},{9,13},{13,17},{17,21},{21,25},{25,29},{4,0},{8,4},{12... | collective-permute-start | bytes 98312 | tf_op jit(solution)/shard_map/ppermute | solution.py:381
  47.2 4.5 %collective-permute-done.13.mine = f32[2,32,128]{2,1,0:T(8,128)S(1)} collective-permute-done((f32[2,32,128]{2,1,0:T(8,128)S(1)}, f32[2,32,128]{2,1,0:T(8,128)S(1)}, u32[]{:S(2)}, u32[]{:S(2)}) %collective-permute-start.13) | collective-permute-done | bytes 32800 | tf_op jit(solution)/shard_map/ppermute | solution.py:381
  51.7 0.0 collective-permute-start.14
  51.8 1.2 %collective-permute-done.14.theirs = f32[2,32,128]{2,1,0:T(8,128)S(1)} collective-permute-done((f32[2,32,128]{2,1,0:T(8,128)S(1)}, f32[2,32,128]{2,1,0:T(8,128)S(1)}, u32[]{:S(2)}, u32[]{:S(2)}) %collective-permute-start.14) | collective-permute-done | bytes 32800 | tf_op jit(solution)/shard_map/ppermute | solution.py:388
  53.0 0.0 collective-permute-done.12.recv
  53.0 2.0 %shard_map.51 = (f32[3,32,32,64]{3,2,1,0:T(8,128)}, f32[32,32,64]{2,1,0:T(8,128)}) custom-call(s32[3]{0:T(128)S(1)} %copy-done.5, f32[4,4,32,128]{3,2,1,0:T(8,128)S(1)} %get-tuple-element.54.keep, f32[4,4,32,128]{3,2,1,0:T(8,128)S(1)} %collective-permute-done.12.recv, f32[2,32,128]{2,1,0:T(8,128)S(1)} %collective-permute-done.13.mine, ...), custom_call_target="tpu_custom_call" | custom-call | bytes 1638400 | tf_op jit(solution)/shard_map/pallas_call | solution.py:282
  (6 shorter events, 0.0 us)
Async XLA Ops:
  0.7 1.9 %copy-start = (bf16[8,1,3,8,64,128]{5,4,3,2,1,0:T(8,128)(2,1)S(1)}, bf16[8,1,3,8,64,128]{5,4,3,2,1,0:T(8,128)(2,1)}, u32[]{:S(2)}) copy-start(bf16[8,1,3,8,64,128]{5,4,3,2,1,0:T(8,128)(2,1)} %own_ref.5) | copy-start | bytes 9437188
  2.6 1.2 %copy-start.3 = (s32[3]{0:T(128)}, s32[3]{0:T(128)S(1)}, u32[]{:S(2)}) copy-start(s32[3]{0:T(128)S(1)} %pad_add_fusion.scal) | copy-start | bytes 40
  2.6 4.0 %copy-start.2 = (bf16[2,256,256]{2,1,0:T(8,128)(2,1)S(1)}, bf16[2,256,256]{2,1,0:T(8,128)(2,1)}, u32[]{:S(2)}) copy-start(bf16[2,256,256]{2,1,0:T(8,128)(2,1)} %constant.14.clone.w_ref) | copy-start | bytes 786436
  3.2 3.4 %collective-permute-start = (bf16[4,1,3,4,64,128]{5,4,3,2,1,0:T(8,128)(2,1)S(1)}, bf16[4,1,3,4,64,128]{5,4,3,2,1,0:T(8,128)(2,1)S(1)}, u32[]{:S(2)}, u32[]{:S(2)}) collective-permute-start(bf16[4,1,3,4,64,128]{5,4,3,2,1,0:T(8,128)(2,1)S(1)} %shard_map.41), channel_id=1, source_target_pairs={{0,1},{1,0},{2,3},{3,2},{4,5},{5,4},{6,7},{7,6},{8,9},{9,8},{10,11... | collective-permute-start | bytes 2359304 | tf_op jit(solution)/shard_map/ppermute | solution.py:339
  6.5 7.1 %collective-permute-start.5 = (bf16[4,1,3,4,64,128]{5,4,3,2,1,0:T(8,128)(2,1)}, bf16[4,1,3,4,64,128]{5,4,3,2,1,0:T(8,128)(2,1)S(1)}, u32[]{:S(2)}, u32[]{:S(2)}) collective-permute-start(bf16[4,1,3,4,64,128]{5,4,3,2,1,0:T(8,128)(2,1)} %shard_map.44), channel_id=1, source_target_pairs={{0,1},{1,0},{2,3},{3,2},{4,5},{5,4},{6,7},{7,6},{8,9},{9,8},{10,11... | collective-permute-start | bytes 2359304 | tf_op jit(solution)/shard_map/ppermute | solution.py:339
  6.6 1.9 %copy-start.1 = (bf16[8,1,3,8,64,128]{5,4,3,2,1,0:T(8,128)(2,1)S(1)}, bf16[8,1,3,8,64,128]{5,4,3,2,1,0:T(8,128)(2,1)}, u32[]{:S(2)}) copy-start(bf16[8,1,3,8,64,128]{5,4,3,2,1,0:T(8,128)(2,1)} %own_ref.5) | copy-start | bytes 9437188
  8.5 0.7 %copy-start.4 = (s32[3]{0:T(128)S(1)}, s32[3]{0:T(128)}, u32[]{:S(2)}) copy-start(s32[3]{0:T(128)} %copy-done.3) | copy-start | bytes 40
  10.6 23.4 %collective-permute-start.1 = (bf16[4,272,128]{2,1,0:T(8,128)(2,1)S(1)}, bf16[4,272,128]{2,1,0:T(8,128)(2,1)S(1)}, u32[]{:S(2)}, u32[]{:S(2)}) collective-permute-start(bf16[4,272,128]{2,1,0:T(8,128)(2,1)S(1)} %get-tuple-element.31), channel_id=1, source_target_pairs={{0,2},{2,0},{1,3},{3,1},{4,6},{6,4},{5,7},{7,5},{8,10},{10,8},{9,1... | collective-permute-start | bytes 835592 | tf_op jit(solution)/shard_map/ppermute | solution.py:353
  14.6 38.4 %copy-start.5 = (s32[3]{0:T(128)S(1)}, s32[3]{0:T(128)}, u32[]{:S(2)}) copy-start(s32[3]{0:T(128)} %copy-done.3) | copy-start | bytes 40
  14.6 9.5 %collective-permute-start.9 = (bf16[2,272,128]{2,1,0:T(8,128)(2,1)S(1)}, bf16[2,272,128]{2,1,0:T(8,128)(2,1)S(1)}, u32[]{:S(2)}, u32[]{:S(2)}) collective-permute-start(bf16[2,272,128]{2,1,0:T(8,128)(2,1)S(1)} %get-tuple-element.43), channel_id=1, source_target_pairs={{0,2},{2,0},{1,3},{3,1},{4,6},{6,4},{5,7},{7,5},{8,10},{10,8},{9,1... | collective-permute-start | bytes 417800 | tf_op jit(solution)/shard_map/ppermute | solution.py:353
  15.6 14.7 %collective-permute-start.6 = (bf16[2,272,128]{2,1,0:T(8,128)(2,1)S(1)}, bf16[2,272,128]{2,1,0:T(8,128)(2,1)S(1)}, u32[]{:S(2)}, u32[]{:S(2)}) collective-permute-start(bf16[2,272,128]{2,1,0:T(8,128)(2,1)S(1)} %get-tuple-element.38), channel_id=1, source_target_pairs={{0,2},{2,0},{1,3},{3,1},{4,6},{6,4},{5,7},{7,5},{8,10},{10,8},{9,1... | collective-permute-start | bytes 417800 | tf_op jit(solution)/shard_map/ppermute | solution.py:353
  25.0 11.8 %collective-permute-start.10 = (bf16[272,128]{1,0:T(8,128)(2,1)S(1)}, bf16[272,128]{1,0:T(8,128)(2,1)S(1)}, u32[]{:S(2)}, u32[]{:S(2)}) collective-permute-start(bf16[272,128]{1,0:T(8,128)(2,1)S(1)} %get-tuple-element.44), channel_id=1, source_target_pairs={{0,24},{4,28},{8,16},{12,20},{16,8},{20,12},{24,0},{28,4},{1,25},{... | collective-permute-start | bytes 208904 | tf_op jit(solution)/shard_map/ppermute | solution.py:363
  29.1 8.9 %collective-permute-start.11 = (bf16[272,128]{1,0:T(8,128)(2,1)S(1)}, bf16[272,128]{1,0:T(8,128)(2,1)S(1)}, u32[]{:S(2)}, u32[]{:S(2)}) collective-permute-start(bf16[272,128]{1,0:T(8,128)(2,1)S(1)} %get-tuple-element.45), channel_id=1, source_target_pairs={{0,28},{4,24},{8,20},{12,16},{16,12},{20,8},{24,4},{28,0},{1,29},{... | collective-permute-start | bytes 208904 | tf_op jit(solution)/shard_map/ppermute | solution.py:363
  31.1 8.1 %collective-permute-start.7 = (bf16[272,128]{1,0:T(8,128)(2,1)S(1)}, bf16[272,128]{1,0:T(8,128)(2,1)S(1)}, u32[]{:S(2)}, u32[]{:S(2)}) collective-permute-start(bf16[272,128]{1,0:T(8,128)(2,1)S(1)} %get-tuple-element.39), channel_id=1, source_target_pairs={{0,16},{4,20},{8,24},{12,28},{16,0},{20,4},{24,8},{28,12},{1,17},{... | collective-permute-start | bytes 208904 | tf_op jit(solution)/shard_map/ppermute | solution.py:363
  32.0 8.1 %collective-permute-start.8 = (bf16[272,128]{1,0:T(8,128)(2,1)S(1)}, bf16[272,128]{1,0:T(8,128)(2,1)S(1)}, u32[]{:S(2)}, u32[]{:S(2)}) collective-permute-start(bf16[272,128]{1,0:T(8,128)(2,1)S(1)} %get-tuple-element.40), channel_id=1, source_target_pairs={{0,20},{4,16},{8,28},{12,24},{16,4},{20,0},{24,12},{28,8},{1,21},{... | collective-permute-start | bytes 208904 | tf_op jit(solution)/shard_map/ppermute | solution.py:363
  35.0 5.9 %collective-permute-start.2 = (bf16[272,128]{1,0:T(8,128)(2,1)S(1)}, bf16[272,128]{1,0:T(8,128)(2,1)S(1)}, u32[]{:S(2)}, u32[]{:S(2)}) collective-permute-start(bf16[272,128]{1,0:T(8,128)(2,1)S(1)} %get-tuple-element.33), channel_id=1, source_target_pairs={{0,4},{4,0},{8,12},{12,8},{16,20},{20,16},{24,28},{28,24},{1,5},{5... | collective-permute-start | bytes 208904 | tf_op jit(solution)/shard_map/ppermute | solution.py:363
  36.7 4.5 %collective-permute-start.3 = (bf16[272,128]{1,0:T(8,128)(2,1)S(1)}, bf16[272,128]{1,0:T(8,128)(2,1)S(1)}, u32[]{:S(2)}, u32[]{:S(2)}) collective-permute-start(bf16[272,128]{1,0:T(8,128)(2,1)S(1)} %get-tuple-element.34), channel_id=1, source_target_pairs={{0,8},{4,12},{8,0},{12,4},{16,24},{20,28},{24,16},{28,20},{1,9},{5... | collective-permute-start | bytes 208904 | tf_op jit(solution)/shard_map/ppermute | solution.py:363
  38.0 5.2 %collective-permute-start.4 = (bf16[272,128]{1,0:T(8,128)(2,1)S(1)}, bf16[272,128]{1,0:T(8,128)(2,1)S(1)}, u32[]{:S(2)}, u32[]{:S(2)}) collective-permute-start(bf16[272,128]{1,0:T(8,128)(2,1)S(1)} %get-tuple-element.35), channel_id=1, source_target_pairs={{0,12},{4,8},{8,4},{12,0},{16,28},{20,24},{24,20},{28,16},{1,13},{... | collective-permute-start | bytes 208904 | tf_op jit(solution)/shard_map/ppermute | solution.py:363
  45.9 7.1 %collective-permute-start.12 = (f32[4,4,32,128]{3,2,1,0:T(8,128)S(1)}, f32[4,4,32,128]{3,2,1,0:T(8,128)S(1)}, u32[]{:S(2)}, u32[]{:S(2)}) collective-permute-start(f32[4,4,32,128]{3,2,1,0:T(8,128)S(1)} %get-tuple-element.55), channel_id=1, source_target_pairs={{0,1},{1,0},{2,3},{3,2},{4,5},{5,4},{6,7},{7,6},{8,9},{9,8},{10,11... | collective-permute-start | bytes 786440 | tf_op jit(solution)/shard_map/ppermute | solution.py:387
  45.9 5.8 %collective-permute-start.13 = (f32[2,32,128]{2,1,0:T(8,128)S(1)}, f32[2,32,128]{2,1,0:T(8,128)S(1)}, u32[]{:S(2)}, u32[]{:S(2)}) collective-permute-start(f32[2,32,128]{2,1,0:T(8,128)S(1)} %shard_map.49), channel_id=1, source_target_pairs={{1,5},{5,9},{9,13},{13,17},{17,21},{21,25},{25,29},{4,0},{8,4},{12... | collective-permute-start | bytes 98312 | tf_op jit(solution)/shard_map/ppermute | solution.py:381
  51.7 1.2 %collective-permute-start.14 = (f32[2,32,128]{2,1,0:T(8,128)S(1)}, f32[2,32,128]{2,1,0:T(8,128)S(1)}, u32[]{:S(2)}, u32[]{:S(2)}) collective-permute-start(f32[2,32,128]{2,1,0:T(8,128)S(1)} %collective-permute-done.13.mine), channel_id=1, source_target_pairs={{0,1},{1,0},{2,3},{3,2},{4,5},{5,4},{6,7},{7,6},{8,9},{9,8},{10,11... | collective-permute-start | bytes 98312 | tf_op jit(solution)/shard_map/ppermute | solution.py:388
where the time goes:
time: 55.3 us; the launch traced here: 55 us
  starting transfers between devices  18.9 us (34%)
  waiting for transfers between devices  16.8 us (30%)
  Pallas kernels  14 us (25%)
  local copies, waits for them, and re-layouts  4.44 us (8%)
  between operations  0.76 us (1%)
    pallas_call x11, Pallas kernels, call(): pl.pallas_call(kernel, out_shape=list(outs), grid_spec=pltpu.PrefetchScal...  14 us
    ppermute x7, starting transfers between devices, messages(): lax.ppermute(p, 'gx', [(i, i ^ s) for i in range(nx_dev)])  11.7 us
    ppermute x3, waiting for transfers between devices, messages(): below = above = lax.ppermute(up, 'gy', [(0, 1), (1, 0)])  6.44 us
    ppermute x3, starting transfers between devices, messages(): below = above = lax.ppermute(up, 'gy', [(0, 1), (1, 0)])  5.2 us
    ppermute x7, waiting for transfers between devices, messages(): lax.ppermute(p, 'gx', [(i, i ^ s) for i in range(nx_dev)])  4.67 us
    ppermute x1, waiting for transfers between devices, stitched(): mine = lax.ppermute(ends, ('gx', 'gz'), above + below)  4.51 us
    unnamed x12, local copies, waits for them, and re-layouts  4.44 us
    ppermute x1, starting transfers between devices, stitched(): mine = lax.ppermute(ends, ('gx', 'gz'), above + below)  1.29 us
  transfers between devices with their start and end apart: 15, of which 8 were waited for; matrix products, arithmetic and copies ran while one was open for 0% of the time, Pallas kernels for 16%

commit v1 on v0

--- a/solution.py
+++ b/solution.py
@@ -324,7 +324,7 @@
     def upper(g, core):
         return ((g * 2 + core) * half >= stride).astype(jnp.int32)
 
-    def swapped(first, mib):
+    def swapped(first):
         def base(g, core):
             start = ((g ^ first) & ~(slabs - 1)) - upper(g, core)
             return jnp.clip(start, 0, positions - slabs)
@@ -334,7 +334,6 @@
             [patches], [like((slabs, 1, 3, half, length, 128), jnp.bfloat16)],
             in_specs=[pl.BlockSpec(memory_space=pl.ANY)],
             scratch=[pltpu.SemaphoreType.DMA(())],
-            mib=mib,
         )
         return lax.ppermute(other, "gz", [(0, 1), (1, 0)]), base
 
@@ -364,8 +363,8 @@
             for s, p in enumerate(parts, first)
         ]
 
-    recv_far = swapped(slabs, 61.5)
-    recv_near = swapped(0, 4)
+    recv_far = swapped(slabs)
+    recv_near = swapped(0)
     first = messages(slabs, slabs // 2, *recv_far)
     second = messages(slabs + slabs // 2, slabs // 2, *recv_far)
     third = messages(0, slabs, *recv_near)

time: 55.3 us -> 51.6 us (0.933)
  local copies, waits for them, and re-layouts: 4.44 us -> 1.89 us
  Pallas kernels: 14 us -> 11.9 us
  waiting for transfers between devices: 16.8 us -> 18 us
    unnamed x12 -> x4, local copies, waits for them, and re-layouts: 4.44 us -> 1.89 us
    pallas_call x11, Pallas kernels: 14 us -> 11.9 us  [call(): pl.pallas_call(kernel, out_shape=list(outs), grid_spec=pltpu.PrefetchScal...]
    ppermute x2, waiting for transfers between devices: 0.01 us -> 1.21 us  [swapped(): return (lax.ppermute(other, 'gz', [(0, 1), (1, 0)]), base)]
  transfers between devices with their start and end apart: 15 -> 15, of which waited for: 8 -> 9; matrix products, arithmetic and copies ran while one was open for 0% -> 0% of each run, Pallas kernels for 16% -> 13%
where the time goes in v1:
time: 51.6 us; the launch traced here: 51.4 us
  starting transfers between devices  18.8 us (36%)
  waiting for transfers between devices  18 us (35%)
  Pallas kernels  11.9 us (23%)
  local copies, waits for them, and re-layouts  1.89 us (4%)
  between operations  0.74 us (1%)
    pallas_call x11, Pallas kernels, call(): pl.pallas_call(kernel, out_shape=list(outs), grid_spec=pltpu.PrefetchScal...  11.9 us
    ppermute x7, starting transfers between devices, messages(): lax.ppermute(p, 'gx', [(i, i ^ s) for i in range(nx_dev)])  11.7 us
    ppermute x3, waiting for transfers between devices, messages(): below = above = lax.ppermute(up, 'gy', [(0, 1), (1, 0)])  6.44 us
    ppermute x3, starting transfers between devices, messages(): below = above = lax.ppermute(up, 'gy', [(0, 1), (1, 0)])  5.09 us
    ppermute x7, waiting for transfers between devices, messages(): lax.ppermute(p, 'gx', [(i, i ^ s) for i in range(nx_dev)])  4.68 us
    ppermute x1, waiting for transfers between devices, stitched(): mine = lax.ppermute(ends, ('gx', 'gz'), above + below)  4.51 us
    unnamed x4, local copies, waits for them, and re-layouts  1.89 us
    ppermute x1, starting transfers between devices, stitched(): mine = lax.ppermute(ends, ('gx', 'gz'), above + below)  1.29 us
  transfers between devices with their start and end apart: 15, of which 9 were waited for; matrix products, arithmetic and copies ran while one was open for 0% of the time, Pallas kernels for 13%

profile of v1, /device:TPU:0, one launch (start us, length us, event | category | flops | bytes accessed | tf_op | source)
XLA Modules:
  0.0 51.4 jit_solution(1993366853905390465)
XLA Ops:
  0.6 0.1 pad_add_fusion.scal
  0.7 0.0 copy-start
  0.7 1.9 %copy-done = bf16[8,1,3,8,64,128]{5,4,3,2,1,0:T(8,128)(2,1)S(1)} copy-done((bf16[8,1,3,8,64,128]{5,4,3,2,1,0:T(8,128)(2,1)S(1)}, bf16[8,1,3,8,64,128]{5,4,3,2,1,0:T(8,128)(2,1)}, u32[]{:S(2)}) %copy-start) | copy-done | bytes 3145752
  2.6 0.0 copy-start.1
  2.6 0.6 %shard_map.41 = bf16[4,1,3,4,64,128]{5,4,3,2,1,0:T(8,128)(2,1)S(1)} custom-call(s32[3]{0:T(128)S(1)} %pad_add_fusion.scal, bf16[8,1,3,8,64,128]{5,4,3,2,1,0:T(8,128)(2,1)S(1)} %copy-done), custom_call_target="tpu_custom_call" | custom-call | bytes 3932160 | tf_op jit(solution)/shard_map/pallas_call | solution.py:282
  3.2 0.6 %collective-permute-start = (bf16[4,1,3,4,64,128]{5,4,3,2,1,0:T(8,128)(2,1)S(1)}, bf16[4,1,3,4,64,128]{5,4,3,2,1,0:T(8,128)(2,1)S(1)}, u32[]{:S(2)}, u32[]{:S(2)}) collective-permute-start(bf16[4,1,3,4,64,128]{5,4,3,2,1,0:T(8,128)(2,1)S(1)} %shard_map.41), channel_id=1, source_target_pairs={{0,1},{1,0},{2,3},{3,2},{4,5},{5,4},{6,7},{7,6},{8,9},{9,8},{10,11... | collective-permute-start | bytes 2359304 | tf_op jit(solution)/shard_map/ppermute | solution.py:338
  3.8 0.6 %shard_map.44 = bf16[4,1,3,4,64,128]{5,4,3,2,1,0:T(8,128)(2,1)S(1)} custom-call(s32[3]{0:T(128)S(1)} %pad_add_fusion.scal, bf16[8,1,3,8,64,128]{5,4,3,2,1,0:T(8,128)(2,1)S(1)} %copy-done), custom_call_target="tpu_custom_call" | custom-call | bytes 3932160 | tf_op jit(solution)/shard_map/pallas_call | solution.py:282
  4.4 0.1 collective-permute-start.5
  4.5 1.2 %collective-permute-done.recv_ref = bf16[4,1,3,4,64,128]{5,4,3,2,1,0:T(8,128)(2,1)S(1)} collective-permute-done((bf16[4,1,3,4,64,128]{5,4,3,2,1,0:T(8,128)(2,1)S(1)}, bf16[4,1,3,4,64,128]{5,4,3,2,1,0:T(8,128)(2,1)S(1)}, u32[]{:S(2)}, u32[]{:S(2)}) %collective-permute-start) | collective-permute-done | bytes 786464 | tf_op jit(solution)/shard_map/ppermute | solution.py:338
  5.7 0.0 copy-done.1
  5.7 1.4 %shard_map.42 = (f32[4,8,32,128]{3,2,1,0:T(8,128)S(1)}, bf16[4,272,128]{2,1,0:T(8,128)(2,1)S(1)}, f32[4,8,128]{2,1,0:T(8,128)S(1)}) custom-call(s32[3]{0:T(128)S(1)} %pad_add_fusion.scal, bf16[8,1,3,8,64,128]{5,4,3,2,1,0:T(8,128)(2,1)S(1)} %copy-done, bf16[4,1,3,4,64,128]{5,4,3,2,1,0:T(8,128)(2,1)S(1)} %collective-permute-done.recv_ref, ...), custom_call_target="tpu_custom_call" | custom-call | bytes 5013504 | tf_op jit(solution)/shard_map/pallas_call | solution.py:282
  7.1 2.9 %collective-permute-start.1 = (bf16[4,272,128]{2,1,0:T(8,128)(2,1)S(1)}, bf16[4,272,128]{2,1,0:T(8,128)(2,1)S(1)}, u32[]{:S(2)}, u32[]{:S(2)}) collective-permute-start(bf16[4,272,128]{2,1,0:T(8,128)(2,1)S(1)} %get-tuple-element.31), channel_id=1, source_target_pairs={{0,2},{2,0},{1,3},{3,1},{4,6},{6,4},{5,7},{7,5},{8,10},{10,8},{9,1... | collective-permute-start | bytes 835592 | tf_op jit(solution)/shard_map/ppermute | solution.py:352
  10.0 0.0 collective-permute-done.5.recv_ref
  10.0 0.9 %shard_map.47 = (f32[2,8,32,128]{3,2,1,0:T(8,128)S(1)}, bf16[2,272,128]{2,1,0:T(8,128)(2,1)S(1)}, f32[2,8,128]{2,1,0:T(8,128)S(1)}) custom-call(s32[3]{0:T(128)S(1)} %pad_add_fusion.scal, bf16[8,1,3,8,64,128]{5,4,3,2,1,0:T(8,128)(2,1)S(1)} %copy-done, bf16[4,1,3,4,64,128]{5,4,3,2,1,0:T(8,128)(2,1)S(1)} %collective-permute-done.5.recv_ref, ...), custom_call_target="tpu_custom_call" | custom-call | bytes 4603904 | tf_op jit(solution)/shard_map/pallas_call | solution.py:282
  11.0 0.1 collective-permute-start.9
  11.1 0.9 %shard_map.45 = (f32[2,8,32,128]{3,2,1,0:T(8,128)S(1)}, bf16[2,272,128]{2,1,0:T(8,128)(2,1)S(1)}, f32[2,8,128]{2,1,0:T(8,128)S(1)}) custom-call(s32[3]{0:T(128)S(1)} %pad_add_fusion.scal, bf16[8,1,3,8,64,128]{5,4,3,2,1,0:T(8,128)(2,1)S(1)} %copy-done, bf16[4,1,3,4,64,128]{5,4,3,2,1,0:T(8,128)(2,1)S(1)} %collective-permute-done.5.recv_ref, ...), custom_call_target="tpu_custom_call" | custom-call | bytes 4603904 | tf_op jit(solution)/shard_map/pallas_call | solution.py:282
  12.0 2.1 %collective-permute-start.6 = (bf16[2,272,128]{2,1,0:T(8,128)(2,1)S(1)}, bf16[2,272,128]{2,1,0:T(8,128)(2,1)S(1)}, u32[]{:S(2)}, u32[]{:S(2)}) collective-permute-start(bf16[2,272,128]{2,1,0:T(8,128)(2,1)S(1)} %get-tuple-element.38), channel_id=1, source_target_pairs={{0,2},{2,0},{1,3},{3,1},{4,6},{6,4},{5,7},{7,5},{8,10},{10,8},{9,1... | collective-permute-start | bytes 417800 | tf_op jit(solution)/shard_map/ppermute | solution.py:352
  14.1 6.4 %collective-permute-done.9.up_ref.down_ref = bf16[2,272,128]{2,1,0:T(8,128)(2,1)S(1)} collective-permute-done((bf16[2,272,128]{2,1,0:T(8,128)(2,1)S(1)}, bf16[2,272,128]{2,1,0:T(8,128)(2,1)S(1)}, u32[]{:S(2)}, u32[]{:S(2)}) %collective-permute-start.9) | collective-permute-done | bytes 139296 | tf_op jit(solution)/shard_map/ppermute | solution.py:352
  20.5 0.9 %shard_map.48 = (bf16[272,128]{1,0:T(8,128)(2,1)S(1)}, bf16[272,128]{1,0:T(8,128)(2,1)S(1)}) custom-call(s32[3]{0:T(128)S(1)} %pad_add_fusion.scal, f32[2,8,32,128]{3,2,1,0:T(8,128)S(1)} %get-tuple-element.41.own_ref, f32[2,8,128]{2,1,0:T(8,128)S(1)} %get-tuple-element.42.next_ref, bf16[2,272,128]{2,1,0:T(8,128)(2,1)S(1)} %collective-permute-done.9.up_ref.down_ref, ...), custom_call_target="tpu_custom_call" | custom-call | bytes 688128 | tf_op jit(solution)/shard_map/pallas_call | solution.py:282
  21.4 4.2 %collective-permute-start.10 = (bf16[272,128]{1,0:T(8,128)(2,1)S(1)}, bf16[272,128]{1,0:T(8,128)(2,1)S(1)}, u32[]{:S(2)}, u32[]{:S(2)}) collective-permute-start(bf16[272,128]{1,0:T(8,128)(2,1)S(1)} %get-tuple-element.44), channel_id=1, source_target_pairs={{0,24},{4,28},{8,16},{12,20},{16,8},{20,12},{24,0},{28,4},{1,25},{... | collective-permute-start | bytes 208904 | tf_op jit(solution)/shard_map/ppermute | solution.py:362
  25.6 1.1 %collective-permute-start.11 = (bf16[272,128]{1,0:T(8,128)(2,1)S(1)}, bf16[272,128]{1,0:T(8,128)(2,1)S(1)}, u32[]{:S(2)}, u32[]{:S(2)}) collective-permute-start(bf16[272,128]{1,0:T(8,128)(2,1)S(1)} %get-tuple-element.45), channel_id=1, source_target_pairs={{0,28},{4,24},{8,20},{12,16},{16,12},{20,8},{24,4},{28,0},{1,29},{... | collective-permute-start | bytes 208904 | tf_op jit(solution)/shard_map/ppermute | solution.py:362
  26.7 0.0 collective-permute-done.6.up_ref.down_ref
  26.7 0.9 %shard_map.46 = (bf16[272,128]{1,0:T(8,128)(2,1)S(1)}, bf16[272,128]{1,0:T(8,128)(2,1)S(1)}) custom-call(s32[3]{0:T(128)S(1)} %pad_add_fusion.scal, f32[2,8,32,128]{3,2,1,0:T(8,128)S(1)} %get-tuple-element.36.own_ref, f32[2,8,128]{2,1,0:T(8,128)S(1)} %get-tuple-element.37.next_ref, bf16[2,272,128]{2,1,0:T(8,128)(2,1)S(1)} %collective-permute-done.6.up_ref.down_ref, ...), custom_call_target="tpu_custom_call" | custom-call | bytes 688128 | tf_op jit(solution)/shard_map/pallas_call | solution.py:282
  27.6 0.9 %collective-permute-start.7 = (bf16[272,128]{1,0:T(8,128)(2,1)S(1)}, bf16[272,128]{1,0:T(8,128)(2,1)S(1)}, u32[]{:S(2)}, u32[]{:S(2)}) collective-permute-start(bf16[272,128]{1,0:T(8,128)(2,1)S(1)} %get-tuple-element.39), channel_id=1, source_target_pairs={{0,16},{4,20},{8,24},{12,28},{16,0},{20,4},{24,8},{28,12},{1,17},{... | collective-permute-start | bytes 208904 | tf_op jit(solution)/shard_map/ppermute | solution.py:362
  28.4 2.0 %collective-permute-start.8 = (bf16[272,128]{1,0:T(8,128)(2,1)S(1)}, bf16[272,128]{1,0:T(8,128)(2,1)S(1)}, u32[]{:S(2)}, u32[]{:S(2)}) collective-permute-start(bf16[272,128]{1,0:T(8,128)(2,1)S(1)} %get-tuple-element.40), channel_id=1, source_target_pairs={{0,20},{4,16},{8,28},{12,24},{16,4},{20,0},{24,12},{28,8},{1,21},{... | collective-permute-start | bytes 208904 | tf_op jit(solution)/shard_map/ppermute | solution.py:362
  30.4 0.0 collective-permute-done.1.up_ref.down_ref
  30.4 1.1 %shard_map.43 = (bf16[272,128]{1,0:T(8,128)(2,1)S(1)}, bf16[272,128]{1,0:T(8,128)(2,1)S(1)}, bf16[272,128]{1,0:T(8,128)(2,1)S(1)}, bf16[272,128]{1,0:T(8,128)(2,1)S(1)}) custom-call(s32[3]{0:T(128)S(1)} %pad_add_fusion.scal, f32[4,8,32,128]{3,2,1,0:T(8,128)S(1)} %get-tuple-element.29.own_ref, f32[4,8,128]{2,1,0:T(8,128)S(1)} %get-tuple-element.30.next_ref, ...), custom_call_target="tpu_custom_call" | custom-call | bytes 1376256 | tf_op jit(solution)/shard_map/pallas_call | solution.py:282
  31.5 1.7 %collective-permute-start.2 = (bf16[272,128]{1,0:T(8,128)(2,1)S(1)}, bf16[272,128]{1,0:T(8,128)(2,1)S(1)}, u32[]{:S(2)}, u32[]{:S(2)}) collective-permute-start(bf16[272,128]{1,0:T(8,128)(2,1)S(1)} %get-tuple-element.33), channel_id=1, source_target_pairs={{0,4},{4,0},{8,12},{12,8},{16,20},{20,16},{24,28},{28,24},{1,5},{5... | collective-permute-start | bytes 208904 | tf_op jit(solution)/shard_map/ppermute | solution.py:362
  33.2 0.0 collective-permute-done.10.refs_6_
  33.2 1.3 %collective-permute-start.3 = (bf16[272,128]{1,0:T(8,128)(2,1)S(1)}, bf16[272,128]{1,0:T(8,128)(2,1)S(1)}, u32[]{:S(2)}, u32[]{:S(2)}) collective-permute-start(bf16[272,128]{1,0:T(8,128)(2,1)S(1)} %get-tuple-element.34), channel_id=1, source_target_pairs={{0,8},{4,12},{8,0},{12,4},{16,24},{20,28},{24,16},{28,20},{1,9},{5... | collective-permute-start | bytes 208904 | tf_op jit(solution)/shard_map/ppermute | solution.py:362
  34.5 0.0 collective-permute-done.11.refs_7_
  34.5 0.5 %collective-permute-start.4 = (bf16[272,128]{1,0:T(8,128)(2,1)S(1)}, bf16[272,128]{1,0:T(8,128)(2,1)S(1)}, u32[]{:S(2)}, u32[]{:S(2)}) collective-permute-start(bf16[272,128]{1,0:T(8,128)(2,1)S(1)} %get-tuple-element.35), channel_id=1, source_target_pairs={{0,12},{4,8},{8,4},{12,0},{16,28},{20,24},{24,20},{28,16},{1,13},{... | collective-permute-start | bytes 208904 | tf_op jit(solution)/shard_map/ppermute | solution.py:362
  35.0 0.8 %collective-permute-done.7.refs_4_ = bf16[272,128]{1,0:T(8,128)(2,1)S(1)} collective-permute-done((bf16[272,128]{1,0:T(8,128)(2,1)S(1)}, bf16[272,128]{1,0:T(8,128)(2,1)S(1)}, u32[]{:S(2)}, u32[]{:S(2)}) %collective-permute-start.7) | collective-permute-done | bytes 69664 | tf_op jit(solution)/shard_map/ppermute | solution.py:362
  35.8 0.8 %collective-permute-done.8.refs_5_ = bf16[272,128]{1,0:T(8,128)(2,1)S(1)} collective-permute-done((bf16[272,128]{1,0:T(8,128)(2,1)S(1)}, bf16[272,128]{1,0:T(8,128)(2,1)S(1)}, u32[]{:S(2)}, u32[]{:S(2)}) %collective-permute-start.8) | collective-permute-done | bytes 69664 | tf_op jit(solution)/shard_map/ppermute | solution.py:362
  36.6 0.9 %collective-permute-done.2.refs_1_ = bf16[272,128]{1,0:T(8,128)(2,1)S(1)} collective-permute-done((bf16[272,128]{1,0:T(8,128)(2,1)S(1)}, bf16[272,128]{1,0:T(8,128)(2,1)S(1)}, u32[]{:S(2)}, u32[]{:S(2)}) %collective-permute-start.2) | collective-permute-done | bytes 69664 | tf_op jit(solution)/shard_map/ppermute | solution.py:362
  37.5 0.5 %collective-permute-done.3.refs_2_ = bf16[272,128]{1,0:T(8,128)(2,1)S(1)} collective-permute-done((bf16[272,128]{1,0:T(8,128)(2,1)S(1)}, bf16[272,128]{1,0:T(8,128)(2,1)S(1)}, u32[]{:S(2)}, u32[]{:S(2)}) %collective-permute-start.3) | collective-permute-done | bytes 69664 | tf_op jit(solution)/shard_map/ppermute | solution.py:362
  38.0 1.7 %collective-permute-done.4.refs_3_ = bf16[272,128]{1,0:T(8,128)(2,1)S(1)} collective-permute-done((bf16[272,128]{1,0:T(8,128)(2,1)S(1)}, bf16[272,128]{1,0:T(8,128)(2,1)S(1)}, u32[]{:S(2)}, u32[]{:S(2)}) %collective-permute-start.4) | collective-permute-done | bytes 69664 | tf_op jit(solution)/shard_map/ppermute | solution.py:362
  39.7 0.8 %shard_map.49 = f32[2,32,128]{2,1,0:T(8,128)S(1)} custom-call(s32[3]{0:T(128)S(1)} %pad_add_fusion.scal, bf16[272,128]{1,0:T(8,128)(2,1)S(1)} %get-tuple-element.46.refs_0_, bf16[272,128]{1,0:T(8,128)(2,1)S(1)} %collective-permute-done.2.refs_1_, bf16[272,128]{1,0:T(8,128)(2,1)S(1)} %collective-permute-done.3.refs_2_, ...), custom_call_target="tpu_custom_call" | custom-call | bytes 589824 | tf_op jit(solution)/shard_map/pallas_call | solution.py:282
  40.5 1.8 %shard_map.50 = (f32[4,4,32,128]{3,2,1,0:T(8,128)S(1)}, f32[4,4,32,128]{3,2,1,0:T(8,128)S(1)}) custom-call(s32[3]{0:T(128)S(1)} %pad_add_fusion.scal, bf16[272,128]{1,0:T(8,128)(2,1)S(1)} %get-tuple-element.46.refs_0_, bf16[272,128]{1,0:T(8,128)(2,1)S(1)} %collective-permute-done.2.refs_1_, bf16[272,128]{1,0:T(8,128)(2,1)S(1)} %collective-permute-done.3.refs_2_, ...), custom_call_target="tpu_custom_call" | custom-call | bytes 1081344 | tf_op jit(solution)/shard_map/pallas_call | solution.py:282
  42.3 0.1 collective-permute-start.12
  42.4 1.3 %collective-permute-start.13 = (f32[2,32,128]{2,1,0:T(8,128)S(1)}, f32[2,32,128]{2,1,0:T(8,128)S(1)}, u32[]{:S(2)}, u32[]{:S(2)}) collective-permute-start(f32[2,32,128]{2,1,0:T(8,128)S(1)} %shard_map.49), channel_id=1, source_target_pairs={{1,5},{5,9},{9,13},{13,17},{17,21},{21,25},{25,29},{4,0},{8,4},{12... | collective-permute-start | bytes 98312 | tf_op jit(solution)/shard_map/ppermute | solution.py:380
  43.7 4.5 %collective-permute-done.13.mine = f32[2,32,128]{2,1,0:T(8,128)S(1)} collective-permute-done((f32[2,32,128]{2,1,0:T(8,128)S(1)}, f32[2,32,128]{2,1,0:T(8,128)S(1)}, u32[]{:S(2)}, u32[]{:S(2)}) %collective-permute-start.13) | collective-permute-done | bytes 32800 | tf_op jit(solution)/shard_map/ppermute | solution.py:380
  48.2 0.0 collective-permute-start.14
  48.2 1.2 %collective-permute-done.14.theirs = f32[2,32,128]{2,1,0:T(8,128)S(1)} collective-permute-done((f32[2,32,128]{2,1,0:T(8,128)S(1)}, f32[2,32,128]{2,1,0:T(8,128)S(1)}, u32[]{:S(2)}, u32[]{:S(2)}) %collective-permute-start.14) | collective-permute-done | bytes 32800 | tf_op jit(solution)/shard_map/ppermute | solution.py:387
  49.4 0.0 collective-permute-done.12.recv
  49.4 2.0 %shard_map.51 = (f32[3,32,32,64]{3,2,1,0:T(8,128)}, f32[32,32,64]{2,1,0:T(8,128)}) custom-call(s32[3]{0:T(128)S(1)} %pad_add_fusion.scal, f32[4,4,32,128]{3,2,1,0:T(8,128)S(1)} %get-tuple-element.54.keep, f32[4,4,32,128]{3,2,1,0:T(8,128)S(1)} %collective-permute-done.12.recv, f32[2,32,128]{2,1,0:T(8,128)S(1)} %collective-permute-done.13.mine, ...), custom_call_target="tpu_custom_call" | custom-call | bytes 1638400 | tf_op jit(solution)/shard_map/pallas_call | solution.py:282
Async XLA Ops:
  0.7 1.9 %copy-start = (bf16[8,1,3,8,64,128]{5,4,3,2,1,0:T(8,128)(2,1)S(1)}, bf16[8,1,3,8,64,128]{5,4,3,2,1,0:T(8,128)(2,1)}, u32[]{:S(2)}) copy-start(bf16[8,1,3,8,64,128]{5,4,3,2,1,0:T(8,128)(2,1)} %own_ref.5) | copy-start | bytes 9437188
  2.6 3.1 %copy-start.1 = (bf16[2,256,256]{2,1,0:T(8,128)(2,1)S(1)}, bf16[2,256,256]{2,1,0:T(8,128)(2,1)}, u32[]{:S(2)}) copy-start(bf16[2,256,256]{2,1,0:T(8,128)(2,1)} %constant.14.clone.w_ref) | copy-start | bytes 786436
  3.2 2.5 %collective-permute-start = (bf16[4,1,3,4,64,128]{5,4,3,2,1,0:T(8,128)(2,1)S(1)}, bf16[4,1,3,4,64,128]{5,4,3,2,1,0:T(8,128)(2,1)S(1)}, u32[]{:S(2)}, u32[]{:S(2)}) collective-permute-start(bf16[4,1,3,4,64,128]{5,4,3,2,1,0:T(8,128)(2,1)S(1)} %shard_map.41), channel_id=1, source_target_pairs={{0,1},{1,0},{2,3},{3,2},{4,5},{5,4},{6,7},{7,6},{8,9},{9,8},{10,11... | collective-permute-start | bytes 2359304 | tf_op jit(solution)/shard_map/ppermute | solution.py:338
  4.4 5.6 %collective-permute-start.5 = (bf16[4,1,3,4,64,128]{5,4,3,2,1,0:T(8,128)(2,1)S(1)}, bf16[4,1,3,4,64,128]{5,4,3,2,1,0:T(8,128)(2,1)S(1)}, u32[]{:S(2)}, u32[]{:S(2)}) collective-permute-start(bf16[4,1,3,4,64,128]{5,4,3,2,1,0:T(8,128)(2,1)S(1)} %shard_map.44), channel_id=1, source_target_pairs={{0,1},{1,0},{2,3},{3,2},{4,5},{5,4},{6,7},{7,6},{8,9},{9,8},{10,11... | collective-permute-start | bytes 2359304 | tf_op jit(solution)/shard_map/ppermute | solution.py:338
  7.1 23.3 %collective-permute-start.1 = (bf16[4,272,128]{2,1,0:T(8,128)(2,1)S(1)}, bf16[4,272,128]{2,1,0:T(8,128)(2,1)S(1)}, u32[]{:S(2)}, u32[]{:S(2)}) collective-permute-start(bf16[4,272,128]{2,1,0:T(8,128)(2,1)S(1)} %get-tuple-element.31), channel_id=1, source_target_pairs={{0,2},{2,0},{1,3},{3,1},{4,6},{6,4},{5,7},{7,5},{8,10},{10,8},{9,1... | collective-permute-start | bytes 835592 | tf_op jit(solution)/shard_map/ppermute | solution.py:352
  11.0 9.5 %collective-permute-start.9 = (bf16[2,272,128]{2,1,0:T(8,128)(2,1)S(1)}, bf16[2,272,128]{2,1,0:T(8,128)(2,1)S(1)}, u32[]{:S(2)}, u32[]{:S(2)}) collective-permute-start(bf16[2,272,128]{2,1,0:T(8,128)(2,1)S(1)} %get-tuple-element.43), channel_id=1, source_target_pairs={{0,2},{2,0},{1,3},{3,1},{4,6},{6,4},{5,7},{7,5},{8,10},{10,8},{9,1... | collective-permute-start | bytes 417800 | tf_op jit(solution)/shard_map/ppermute | solution.py:352
  12.0 14.7 %collective-permute-start.6 = (bf16[2,272,128]{2,1,0:T(8,128)(2,1)S(1)}, bf16[2,272,128]{2,1,0:T(8,128)(2,1)S(1)}, u32[]{:S(2)}, u32[]{:S(2)}) collective-permute-start(bf16[2,272,128]{2,1,0:T(8,128)(2,1)S(1)} %get-tuple-element.38), channel_id=1, source_target_pairs={{0,2},{2,0},{1,3},{3,1},{4,6},{6,4},{5,7},{7,5},{8,10},{10,8},{9,1... | collective-permute-start | bytes 417800 | tf_op jit(solution)/shard_map/ppermute | solution.py:352
  21.4 11.8 %collective-permute-start.10 = (bf16[272,128]{1,0:T(8,128)(2,1)S(1)}, bf16[272,128]{1,0:T(8,128)(2,1)S(1)}, u32[]{:S(2)}, u32[]{:S(2)}) collective-permute-start(bf16[272,128]{1,0:T(8,128)(2,1)S(1)} %get-tuple-element.44), channel_id=1, source_target_pairs={{0,24},{4,28},{8,16},{12,20},{16,8},{20,12},{24,0},{28,4},{1,25},{... | collective-permute-start | bytes 208904 | tf_op jit(solution)/shard_map/ppermute | solution.py:362
  25.6 8.9 %collective-permute-start.11 = (bf16[272,128]{1,0:T(8,128)(2,1)S(1)}, bf16[272,128]{1,0:T(8,128)(2,1)S(1)}, u32[]{:S(2)}, u32[]{:S(2)}) collective-permute-start(bf16[272,128]{1,0:T(8,128)(2,1)S(1)} %get-tuple-element.45), channel_id=1, source_target_pairs={{0,28},{4,24},{8,20},{12,16},{16,12},{20,8},{24,4},{28,0},{1,29},{... | collective-permute-start | bytes 208904 | tf_op jit(solution)/shard_map/ppermute | solution.py:362
  27.6 8.2 %collective-permute-start.7 = (bf16[272,128]{1,0:T(8,128)(2,1)S(1)}, bf16[272,128]{1,0:T(8,128)(2,1)S(1)}, u32[]{:S(2)}, u32[]{:S(2)}) collective-permute-start(bf16[272,128]{1,0:T(8,128)(2,1)S(1)} %get-tuple-element.39), channel_id=1, source_target_pairs={{0,16},{4,20},{8,24},{12,28},{16,0},{20,4},{24,8},{28,12},{1,17},{... | collective-permute-start | bytes 208904 | tf_op jit(solution)/shard_map/ppermute | solution.py:362
  28.4 8.1 %collective-permute-start.8 = (bf16[272,128]{1,0:T(8,128)(2,1)S(1)}, bf16[272,128]{1,0:T(8,128)(2,1)S(1)}, u32[]{:S(2)}, u32[]{:S(2)}) collective-permute-start(bf16[272,128]{1,0:T(8,128)(2,1)S(1)} %get-tuple-element.40), channel_id=1, source_target_pairs={{0,20},{4,16},{8,28},{12,24},{16,4},{20,0},{24,12},{28,8},{1,21},{... | collective-permute-start | bytes 208904 | tf_op jit(solution)/shard_map/ppermute | solution.py:362
  31.5 6.0 %collective-permute-start.2 = (bf16[272,128]{1,0:T(8,128)(2,1)S(1)}, bf16[272,128]{1,0:T(8,128)(2,1)S(1)}, u32[]{:S(2)}, u32[]{:S(2)}) collective-permute-start(bf16[272,128]{1,0:T(8,128)(2,1)S(1)} %get-tuple-element.33), channel_id=1, source_target_pairs={{0,4},{4,0},{8,12},{12,8},{16,20},{20,16},{24,28},{28,24},{1,5},{5... | collective-permute-start | bytes 208904 | tf_op jit(solution)/shard_map/ppermute | solution.py:362
  33.2 4.9 %collective-permute-start.3 = (bf16[272,128]{1,0:T(8,128)(2,1)S(1)}, bf16[272,128]{1,0:T(8,128)(2,1)S(1)}, u32[]{:S(2)}, u32[]{:S(2)}) collective-permute-start(bf16[272,128]{1,0:T(8,128)(2,1)S(1)} %get-tuple-element.34), channel_id=1, source_target_pairs={{0,8},{4,12},{8,0},{12,4},{16,24},{20,28},{24,16},{28,20},{1,9},{5... | collective-permute-start | bytes 208904 | tf_op jit(solution)/shard_map/ppermute | solution.py:362
  34.5 5.2 %collective-permute-start.4 = (bf16[272,128]{1,0:T(8,128)(2,1)S(1)}, bf16[272,128]{1,0:T(8,128)(2,1)S(1)}, u32[]{:S(2)}, u32[]{:S(2)}) collective-permute-start(bf16[272,128]{1,0:T(8,128)(2,1)S(1)} %get-tuple-element.35), channel_id=1, source_target_pairs={{0,12},{4,8},{8,4},{12,0},{16,28},{20,24},{24,20},{28,16},{1,13},{... | collective-permute-start | bytes 208904 | tf_op jit(solution)/shard_map/ppermute | solution.py:362
  42.3 7.1 %collective-permute-start.12 = (f32[4,4,32,128]{3,2,1,0:T(8,128)S(1)}, f32[4,4,32,128]{3,2,1,0:T(8,128)S(1)}, u32[]{:S(2)}, u32[]{:S(2)}) collective-permute-start(f32[4,4,32,128]{3,2,1,0:T(8,128)S(1)} %get-tuple-element.55), channel_id=1, source_target_pairs={{0,1},{1,0},{2,3},{3,2},{4,5},{5,4},{6,7},{7,6},{8,9},{9,8},{10,11... | collective-permute-start | bytes 786440 | tf_op jit(solution)/shard_map/ppermute | solution.py:386
  42.4 5.8 %collective-permute-start.13 = (f32[2,32,128]{2,1,0:T(8,128)S(1)}, f32[2,32,128]{2,1,0:T(8,128)S(1)}, u32[]{:S(2)}, u32[]{:S(2)}) collective-permute-start(f32[2,32,128]{2,1,0:T(8,128)S(1)} %shard_map.49), channel_id=1, source_target_pairs={{1,5},{5,9},{9,13},{13,17},{17,21},{21,25},{25,29},{4,0},{8,4},{12... | collective-permute-start | bytes 98312 | tf_op jit(solution)/shard_map/ppermute | solution.py:380
  48.2 1.2 %collective-permute-start.14 = (f32[2,32,128]{2,1,0:T(8,128)S(1)}, f32[2,32,128]{2,1,0:T(8,128)S(1)}, u32[]{:S(2)}, u32[]{:S(2)}) collective-permute-start(f32[2,32,128]{2,1,0:T(8,128)S(1)} %collective-permute-done.13.mine), channel_id=1, source_target_pairs={{0,1},{1,0},{2,3},{3,2},{4,5},{5,4},{6,7},{7,6},{8,9},{9,8},{10,11... | collective-permute-start | bytes 98312 | tf_op jit(solution)/shard_map/ppermute | solution.py:387

commit v2 on v1

--- a/solution.py
+++ b/solution.py
@@ -1,4 +1,5 @@
 import functools
+import math
 
 import jax
 import jax.numpy as jnp
@@ -278,7 +279,7 @@
 def call(kernel, scal, args, outs, in_specs=None, out_specs=None, grid=(1,), scratch=(),
          mib=4, flops=0):
     args = list(args)
-    size = sum(a.size * a.dtype.itemsize for a in args + list(outs))
+    size = sum(math.prod(a.shape) * a.dtype.itemsize for a in args + list(outs))
     return pl.pallas_call(
         kernel,
         out_shape=list(outs),
@@ -329,10 +330,13 @@
             start = ((g ^ first) & ~(slabs - 1)) - upper(g, core)
             return jnp.clip(start, 0, positions - slabs)
 
+        shape = (slabs, 1, 3, half, length, 128)
         (other,) = call(
             functools.partial(pick_kernel, dict(dims, count=slabs, base=base)), scal,
-            [patches], [like((slabs, 1, 3, half, length, 128), jnp.bfloat16)],
+            [pltpu.with_memory_space_constraint(patches, pltpu.HBM) if first else patches],
+            [pltpu.VMEM(shape, jnp.bfloat16)],
             in_specs=[pl.BlockSpec(memory_space=pl.ANY)],
+            out_specs=[pl.BlockSpec(memory_space=pltpu.VMEM)],
             scratch=[pltpu.SemaphoreType.DMA(())],
         )
         return lax.ppermute(other, "gz", [(0, 1), (1, 0)]), base

time: 51.6 us -> 51.6 us (level)
  waiting for transfers between devices: 18 us -> 16.3 us
  Pallas kernels: 11.9 us -> 13 us
  starting transfers between devices: 18.8 us -> 19.5 us
    ppermute x2, waiting for transfers between devices: 1.21 us -> 0.13 us  [swapped(): return (lax.ppermute(other, 'gz', [(0, 1), (1, 0)]), base)]
    pallas_call x11, Pallas kernels: 11.9 us -> 13 us  [call(): pl.pallas_call(kernel, out_shape=list(outs), grid_spec=pltpu.PrefetchScal...]
    ppermute x7, starting transfers between devices: 11.7 us -> 12.4 us  [messages(): lax.ppermute(p, 'gx', [(i, i ^ s) for i in range(nx_dev)])]
    ppermute x7, waiting for transfers between devices: 4.68 us -> 3.99 us  [messages(): lax.ppermute(p, 'gx', [(i, i ^ s) for i in range(nx_dev)])]
    unnamed x4 -> x6, local copies, waits for them, and re-layouts: 1.89 us -> 1.9 us
  transfers between devices with their start and end apart: 15 -> 15, of which waited for: 9 -> 9; matrix products, arithmetic and copies ran while one was open for 0% -> 0% of each run, Pallas kernels for 13% -> 15%
where the time goes in v2:
time: 51.6 us; the launch traced here: 51.4 us
  starting transfers between devices  19.5 us (38%)
  waiting for transfers between devices  16.3 us (32%)
  Pallas kernels  13 us (25%)
  local copies, waits for them, and re-layouts  1.9 us (4%)
  between operations  0.74 us (1%)
    pallas_call x11, Pallas kernels, call(): pl.pallas_call(kernel, out_shape=list(outs), grid_spec=pltpu.PrefetchScal...  13 us
    ppermute x7, starting transfers between devices, messages(): lax.ppermute(p, 'gx', [(i, i ^ s) for i in range(nx_dev)])  12.4 us
    ppermute x3, waiting for transfers between devices, messages(): below = above = lax.ppermute(up, 'gy', [(0, 1), (1, 0)])  6.44 us
    ppermute x3, starting transfers between devices, messages(): below = above = lax.ppermute(up, 'gy', [(0, 1), (1, 0)])  5.1 us
    ppermute x1, waiting for transfers between devices, stitched(): mine = lax.ppermute(ends, ('gx', 'gz'), above + below)  4.51 us
    ppermute x7, waiting for transfers between devices, messages(): lax.ppermute(p, 'gx', [(i, i ^ s) for i in range(nx_dev)])  3.99 us
    unnamed x6, local copies, waits for them, and re-layouts  1.9 us
    ppermute x1, starting transfers between devices, stitched(): mine = lax.ppermute(ends, ('gx', 'gz'), above + below)  1.29 us
  transfers between devices with their start and end apart: 15, of which 9 were waited for; matrix products, arithmetic and copies ran while one was open for 0% of the time, Pallas kernels for 15%

profile of v2, /device:TPU:0, one launch (start us, length us, event | category | flops | bytes accessed | tf_op | source)
XLA Modules:
  0.0 51.4 jit_solution(7061359105256366164)
XLA Ops:
  0.6 0.1 pad_add_fusion.scal
  0.7 0.0 copy-start
  0.7 1.9 %copy-done = bf16[8,1,3,8,64,128]{5,4,3,2,1,0:T(8,128)(2,1)S(1)} copy-done((bf16[8,1,3,8,64,128]{5,4,3,2,1,0:T(8,128)(2,1)S(1)}, bf16[8,1,3,8,64,128]{5,4,3,2,1,0:T(8,128)(2,1)}, u32[]{:S(2)}) %copy-start) | copy-done | bytes 3145752
  2.6 0.0 copy-start.1
  2.6 0.0 copy-start.2
  2.6 0.6 %shard_map.41 = bf16[4,1,3,4,64,128]{5,4,3,2,1,0:T(8,128)(2,1)S(1)} custom-call(s32[3]{0:T(128)S(1)} %pad_add_fusion.scal, bf16[8,1,3,8,64,128]{5,4,3,2,1,0:T(8,128)(2,1)S(1)} %copy-done), custom_call_target="tpu_custom_call" | custom-call | bytes 3932160 | tf_op jit(solution)/shard_map/pallas_call | solution.py:283
  3.2 0.6 %collective-permute-start = (bf16[4,1,3,4,64,128]{5,4,3,2,1,0:T(8,128)(2,1)S(1)}, bf16[4,1,3,4,64,128]{5,4,3,2,1,0:T(8,128)(2,1)S(1)}, u32[]{:S(2)}, u32[]{:S(2)}) collective-permute-start(bf16[4,1,3,4,64,128]{5,4,3,2,1,0:T(8,128)(2,1)S(1)} %shard_map.41), channel_id=1, source_target_pairs={{0,1},{1,0},{2,3},{3,2},{4,5},{5,4},{6,7},{7,6},{8,9},{9,8},{10,11... | collective-permute-start | bytes 2359304 | tf_op jit(solution)/shard_map/ppermute | solution.py:342
  3.8 1.7 %shard_map.44 = bf16[4,1,3,4,64,128]{5,4,3,2,1,0:T(8,128)(2,1)S(1)} custom-call(s32[3]{0:T(128)S(1)} %pad_add_fusion.scal, bf16[8,1,3,8,64,128]{5,4,3,2,1,0:T(8,128)(2,1)} %own_ref.5), custom_call_target="tpu_custom_call" | custom-call | bytes 3932160 | tf_op jit(solution)/shard_map/pallas_call | solution.py:283
  5.5 0.1 collective-permute-start.5
  5.6 0.1 collective-permute-done.recv_ref
  5.7 0.0 copy-done.1
  5.7 0.0 copy-done.2
  5.7 1.4 %shard_map.42 = (f32[4,8,32,128]{3,2,1,0:T(8,128)S(1)}, bf16[4,272,128]{2,1,0:T(8,128)(2,1)S(1)}, f32[4,8,128]{2,1,0:T(8,128)S(1)}) custom-call(s32[3]{0:T(128)S(1)} %pad_add_fusion.scal, bf16[8,1,3,8,64,128]{5,4,3,2,1,0:T(8,128)(2,1)S(1)} %copy-done.1, bf16[4,1,3,4,64,128]{5,4,3,2,1,0:T(8,128)(2,1)S(1)} %collective-permute-done.recv_ref, ...), custom_call_target="tpu_custom_call" | custom-call | bytes 5013504 | tf_op jit(solution)/shard_map/pallas_call | solution.py:283
  7.1 2.9 %collective-permute-start.1 = (bf16[4,272,128]{2,1,0:T(8,128)(2,1)S(1)}, bf16[4,272,128]{2,1,0:T(8,128)(2,1)S(1)}, u32[]{:S(2)}, u32[]{:S(2)}) collective-permute-start(bf16[4,272,128]{2,1,0:T(8,128)(2,1)S(1)} %get-tuple-element.31), channel_id=1, source_target_pairs={{0,2},{2,0},{1,3},{3,1},{4,6},{6,4},{5,7},{7,5},{8,10},{10,8},{9,1... | collective-permute-start | bytes 835592 | tf_op jit(solution)/shard_map/ppermute | solution.py:356
  10.0 0.0 collective-permute-done.5.recv_ref
  10.0 0.9 %shard_map.47 = (f32[2,8,32,128]{3,2,1,0:T(8,128)S(1)}, bf16[2,272,128]{2,1,0:T(8,128)(2,1)S(1)}, f32[2,8,128]{2,1,0:T(8,128)S(1)}) custom-call(s32[3]{0:T(128)S(1)} %pad_add_fusion.scal, bf16[8,1,3,8,64,128]{5,4,3,2,1,0:T(8,128)(2,1)S(1)} %copy-done.1, bf16[4,1,3,4,64,128]{5,4,3,2,1,0:T(8,128)(2,1)S(1)} %collective-permute-done.5.recv_ref, ...), custom_call_target="tpu_custom_call" | custom-call | bytes 4603904 | tf_op jit(solution)/shard_map/pallas_call | solution.py:283
  11.0 0.5 collective-permute-start.9
  11.5 0.9 %shard_map.45 = (f32[2,8,32,128]{3,2,1,0:T(8,128)S(1)}, bf16[2,272,128]{2,1,0:T(8,128)(2,1)S(1)}, f32[2,8,128]{2,1,0:T(8,128)S(1)}) custom-call(s32[3]{0:T(128)S(1)} %pad_add_fusion.scal, bf16[8,1,3,8,64,128]{5,4,3,2,1,0:T(8,128)(2,1)S(1)} %copy-done.1, bf16[4,1,3,4,64,128]{5,4,3,2,1,0:T(8,128)(2,1)S(1)} %collective-permute-done.5.recv_ref, ...), custom_call_target="tpu_custom_call" | custom-call | bytes 4603904 | tf_op jit(solution)/shard_map/pallas_call | solution.py:283
  12.4 1.7 %collective-permute-start.6 = (bf16[2,272,128]{2,1,0:T(8,128)(2,1)S(1)}, bf16[2,272,128]{2,1,0:T(8,128)(2,1)S(1)}, u32[]{:S(2)}, u32[]{:S(2)}) collective-permute-start(bf16[2,272,128]{2,1,0:T(8,128)(2,1)S(1)} %get-tuple-element.38), channel_id=1, source_target_pairs={{0,2},{2,0},{1,3},{3,1},{4,6},{6,4},{5,7},{7,5},{8,10},{10,8},{9,1... | collective-permute-start | bytes 417800 | tf_op jit(solution)/shard_map/ppermute | solution.py:356
  14.1 6.4 %collective-permute-done.9.up_ref.down_ref = bf16[2,272,128]{2,1,0:T(8,128)(2,1)S(1)} collective-permute-done((bf16[2,272,128]{2,1,0:T(8,128)(2,1)S(1)}, bf16[2,272,128]{2,1,0:T(8,128)(2,1)S(1)}, u32[]{:S(2)}, u32[]{:S(2)}) %collective-permute-start.9) | collective-permute-done | bytes 139296 | tf_op jit(solution)/shard_map/ppermute | solution.py:356
  20.5 0.9 %shard_map.48 = (bf16[272,128]{1,0:T(8,128)(2,1)S(1)}, bf16[272,128]{1,0:T(8,128)(2,1)S(1)}) custom-call(s32[3]{0:T(128)S(1)} %pad_add_fusion.scal, f32[2,8,32,128]{3,2,1,0:T(8,128)S(1)} %get-tuple-element.41.own_ref, f32[2,8,128]{2,1,0:T(8,128)S(1)} %get-tuple-element.42.next_ref, bf16[2,272,128]{2,1,0:T(8,128)(2,1)S(1)} %collective-permute-done.9.up_ref.down_ref, ...), custom_call_target="tpu_custom_call" | custom-call | bytes 688128 | tf_op jit(solution)/shard_map/pallas_call | solution.py:283
  21.4 4.2 %collective-permute-start.10 = (bf16[272,128]{1,0:T(8,128)(2,1)S(1)}, bf16[272,128]{1,0:T(8,128)(2,1)S(1)}, u32[]{:S(2)}, u32[]{:S(2)}) collective-permute-start(bf16[272,128]{1,0:T(8,128)(2,1)S(1)} %get-tuple-element.44), channel_id=1, source_target_pairs={{0,24},{4,28},{8,16},{12,20},{16,8},{20,12},{24,0},{28,4},{1,25},{... | collective-permute-start | bytes 208904 | tf_op jit(solution)/shard_map/ppermute | solution.py:366
  25.6 1.1 %collective-permute-start.11 = (bf16[272,128]{1,0:T(8,128)(2,1)S(1)}, bf16[272,128]{1,0:T(8,128)(2,1)S(1)}, u32[]{:S(2)}, u32[]{:S(2)}) collective-permute-start(bf16[272,128]{1,0:T(8,128)(2,1)S(1)} %get-tuple-element.45), channel_id=1, source_target_pairs={{0,28},{4,24},{8,20},{12,16},{16,12},{20,8},{24,4},{28,0},{1,29},{... | collective-permute-start | bytes 208904 | tf_op jit(solution)/shard_map/ppermute | solution.py:366
  26.7 0.0 collective-permute-done.6.up_ref.down_ref
  26.7 0.9 %shard_map.46 = (bf16[272,128]{1,0:T(8,128)(2,1)S(1)}, bf16[272,128]{1,0:T(8,128)(2,1)S(1)}) custom-call(s32[3]{0:T(128)S(1)} %pad_add_fusion.scal, f32[2,8,32,128]{3,2,1,0:T(8,128)S(1)} %get-tuple-element.36.own_ref, f32[2,8,128]{2,1,0:T(8,128)S(1)} %get-tuple-element.37.next_ref, bf16[2,272,128]{2,1,0:T(8,128)(2,1)S(1)} %collective-permute-done.6.up_ref.down_ref, ...), custom_call_target="tpu_custom_call" | custom-call | bytes 688128 | tf_op jit(solution)/shard_map/pallas_call | solution.py:283
  27.6 0.9 %collective-permute-start.7 = (bf16[272,128]{1,0:T(8,128)(2,1)S(1)}, bf16[272,128]{1,0:T(8,128)(2,1)S(1)}, u32[]{:S(2)}, u32[]{:S(2)}) collective-permute-start(bf16[272,128]{1,0:T(8,128)(2,1)S(1)} %get-tuple-element.39), channel_id=1, source_target_pairs={{0,16},{4,20},{8,24},{12,28},{16,0},{20,4},{24,8},{28,12},{1,17},{... | collective-permute-start | bytes 208904 | tf_op jit(solution)/shard_map/ppermute | solution.py:366
  28.5 2.0 %collective-permute-start.8 = (bf16[272,128]{1,0:T(8,128)(2,1)S(1)}, bf16[272,128]{1,0:T(8,128)(2,1)S(1)}, u32[]{:S(2)}, u32[]{:S(2)}) collective-permute-start(bf16[272,128]{1,0:T(8,128)(2,1)S(1)} %get-tuple-element.40), channel_id=1, source_target_pairs={{0,20},{4,16},{8,28},{12,24},{16,4},{20,0},{24,12},{28,8},{1,21},{... | collective-permute-start | bytes 208904 | tf_op jit(solution)/shard_map/ppermute | solution.py:366
  30.4 0.0 collective-permute-done.1.up_ref.down_ref
  30.4 1.1 %shard_map.43 = (bf16[272,128]{1,0:T(8,128)(2,1)S(1)}, bf16[272,128]{1,0:T(8,128)(2,1)S(1)}, bf16[272,128]{1,0:T(8,128)(2,1)S(1)}, bf16[272,128]{1,0:T(8,128)(2,1)S(1)}) custom-call(s32[3]{0:T(128)S(1)} %pad_add_fusion.scal, f32[4,8,32,128]{3,2,1,0:T(8,128)S(1)} %get-tuple-element.29.own_ref, f32[4,8,128]{2,1,0:T(8,128)S(1)} %get-tuple-element.30.next_ref, ...), custom_call_target="tpu_custom_call" | custom-call | bytes 1376256 | tf_op jit(solution)/shard_map/pallas_call | solution.py:283
  31.5 1.7 %collective-permute-start.2 = (bf16[272,128]{1,0:T(8,128)(2,1)S(1)}, bf16[272,128]{1,0:T(8,128)(2,1)S(1)}, u32[]{:S(2)}, u32[]{:S(2)}) collective-permute-start(bf16[272,128]{1,0:T(8,128)(2,1)S(1)} %get-tuple-element.33), channel_id=1, source_target_pairs={{0,4},{4,0},{8,12},{12,8},{16,20},{20,16},{24,28},{28,24},{1,5},{5... | collective-permute-start | bytes 208904 | tf_op jit(solution)/shard_map/ppermute | solution.py:366
  33.2 0.0 collective-permute-done.10.refs_6_
  33.2 1.3 %collective-permute-start.3 = (bf16[272,128]{1,0:T(8,128)(2,1)S(1)}, bf16[272,128]{1,0:T(8,128)(2,1)S(1)}, u32[]{:S(2)}, u32[]{:S(2)}) collective-permute-start(bf16[272,128]{1,0:T(8,128)(2,1)S(1)} %get-tuple-element.34), channel_id=1, source_target_pairs={{0,8},{4,12},{8,0},{12,4},{16,24},{20,28},{24,16},{28,20},{1,9},{5... | collective-permute-start | bytes 208904 | tf_op jit(solution)/shard_map/ppermute | solution.py:366
  34.5 0.0 collective-permute-done.11.refs_7_
  34.5 1.2 %collective-permute-start.4 = (bf16[272,128]{1,0:T(8,128)(2,1)S(1)}, bf16[272,128]{1,0:T(8,128)(2,1)S(1)}, u32[]{:S(2)}, u32[]{:S(2)}) collective-permute-start(bf16[272,128]{1,0:T(8,128)(2,1)S(1)} %get-tuple-element.35), channel_id=1, source_target_pairs={{0,12},{4,8},{8,4},{12,0},{16,28},{20,24},{24,20},{28,16},{1,13},{... | collective-permute-start | bytes 208904 | tf_op jit(solution)/shard_map/ppermute | solution.py:366
  35.7 0.1 collective-permute-done.7.refs_4_
  35.9 0.7 %collective-permute-done.8.refs_5_ = bf16[272,128]{1,0:T(8,128)(2,1)S(1)} collective-permute-done((bf16[272,128]{1,0:T(8,128)(2,1)S(1)}, bf16[272,128]{1,0:T(8,128)(2,1)S(1)}, u32[]{:S(2)}, u32[]{:S(2)}) %collective-permute-start.8) | collective-permute-done | bytes 69664 | tf_op jit(solution)/shard_map/ppermute | solution.py:366
  36.6 0.9 %collective-permute-done.2.refs_1_ = bf16[272,128]{1,0:T(8,128)(2,1)S(1)} collective-permute-done((bf16[272,128]{1,0:T(8,128)(2,1)S(1)}, bf16[272,128]{1,0:T(8,128)(2,1)S(1)}, u32[]{:S(2)}, u32[]{:S(2)}) %collective-permute-start.2) | collective-permute-done | bytes 69664 | tf_op jit(solution)/shard_map/ppermute | solution.py:366
  37.5 0.5 %collective-permute-done.3.refs_2_ = bf16[272,128]{1,0:T(8,128)(2,1)S(1)} collective-permute-done((bf16[272,128]{1,0:T(8,128)(2,1)S(1)}, bf16[272,128]{1,0:T(8,128)(2,1)S(1)}, u32[]{:S(2)}, u32[]{:S(2)}) %collective-permute-start.3) | collective-permute-done | bytes 69664 | tf_op jit(solution)/shard_map/ppermute | solution.py:366
  38.0 1.7 %collective-permute-done.4.refs_3_ = bf16[272,128]{1,0:T(8,128)(2,1)S(1)} collective-permute-done((bf16[272,128]{1,0:T(8,128)(2,1)S(1)}, bf16[272,128]{1,0:T(8,128)(2,1)S(1)}, u32[]{:S(2)}, u32[]{:S(2)}) %collective-permute-start.4) | collective-permute-done | bytes 69664 | tf_op jit(solution)/shard_map/ppermute | solution.py:366
  39.7 0.8 %shard_map.49 = f32[2,32,128]{2,1,0:T(8,128)S(1)} custom-call(s32[3]{0:T(128)S(1)} %pad_add_fusion.scal, bf16[272,128]{1,0:T(8,128)(2,1)S(1)} %get-tuple-element.46.refs_0_, bf16[272,128]{1,0:T(8,128)(2,1)S(1)} %collective-permute-done.2.refs_1_, bf16[272,128]{1,0:T(8,128)(2,1)S(1)} %collective-permute-done.3.refs_2_, ...), custom_call_target="tpu_custom_call" | custom-call | bytes 589824 | tf_op jit(solution)/shard_map/pallas_call | solution.py:283
  40.5 1.8 %shard_map.50 = (f32[4,4,32,128]{3,2,1,0:T(8,128)S(1)}, f32[4,4,32,128]{3,2,1,0:T(8,128)S(1)}) custom-call(s32[3]{0:T(128)S(1)} %pad_add_fusion.scal, bf16[272,128]{1,0:T(8,128)(2,1)S(1)} %get-tuple-element.46.refs_0_, bf16[272,128]{1,0:T(8,128)(2,1)S(1)} %collective-permute-done.2.refs_1_, bf16[272,128]{1,0:T(8,128)(2,1)S(1)} %collective-permute-done.3.refs_2_, ...), custom_call_target="tpu_custom_call" | custom-call | bytes 1081344 | tf_op jit(solution)/shard_map/pallas_call | solution.py:283
  42.3 0.1 collective-permute-start.12
  42.4 1.3 %collective-permute-start.13 = (f32[2,32,128]{2,1,0:T(8,128)S(1)}, f32[2,32,128]{2,1,0:T(8,128)S(1)}, u32[]{:S(2)}, u32[]{:S(2)}) collective-permute-start(f32[2,32,128]{2,1,0:T(8,128)S(1)} %shard_map.49), channel_id=1, source_target_pairs={{1,5},{5,9},{9,13},{13,17},{17,21},{21,25},{25,29},{4,0},{8,4},{12... | collective-permute-start | bytes 98312 | tf_op jit(solution)/shard_map/ppermute | solution.py:384
  43.7 4.5 %collective-permute-done.13.mine = f32[2,32,128]{2,1,0:T(8,128)S(1)} collective-permute-done((f32[2,32,128]{2,1,0:T(8,128)S(1)}, f32[2,32,128]{2,1,0:T(8,128)S(1)}, u32[]{:S(2)}, u32[]{:S(2)}) %collective-permute-start.13) | collective-permute-done | bytes 32800 | tf_op jit(solution)/shard_map/ppermute | solution.py:384
  48.2 0.0 collective-permute-start.14
  48.2 1.2 %collective-permute-done.14.theirs = f32[2,32,128]{2,1,0:T(8,128)S(1)} collective-permute-done((f32[2,32,128]{2,1,0:T(8,128)S(1)}, f32[2,32,128]{2,1,0:T(8,128)S(1)}, u32[]{:S(2)}, u32[]{:S(2)}) %collective-permute-start.14) | collective-permute-done | bytes 32800 | tf_op jit(solution)/shard_map/ppermute | solution.py:391
  49.4 0.0 collective-permute-done.12.recv
  49.4 2.0 %shard_map.51 = (f32[3,32,32,64]{3,2,1,0:T(8,128)}, f32[32,32,64]{2,1,0:T(8,128)}) custom-call(s32[3]{0:T(128)S(1)} %pad_add_fusion.scal, f32[4,4,32,128]{3,2,1,0:T(8,128)S(1)} %get-tuple-element.54.keep, f32[4,4,32,128]{3,2,1,0:T(8,128)S(1)} %collective-permute-done.12.recv, f32[2,32,128]{2,1,0:T(8,128)S(1)} %collective-permute-done.13.mine, ...), custom_call_target="tpu_custom_call" | custom-call | bytes 1638400 | tf_op jit(solution)/shard_map/pallas_call | solution.py:283
Async XLA Ops:
  0.7 1.9 %copy-start = (bf16[8,1,3,8,64,128]{5,4,3,2,1,0:T(8,128)(2,1)S(1)}, bf16[8,1,3,8,64,128]{5,4,3,2,1,0:T(8,128)(2,1)}, u32[]{:S(2)}) copy-start(bf16[8,1,3,8,64,128]{5,4,3,2,1,0:T(8,128)(2,1)} %own_ref.5) | copy-start | bytes 9437188
  2.6 3.1 %copy-start.1 = (bf16[8,1,3,8,64,128]{5,4,3,2,1,0:T(8,128)(2,1)S(1)}, bf16[8,1,3,8,64,128]{5,4,3,2,1,0:T(8,128)(2,1)}, u32[]{:S(2)}) copy-start(bf16[8,1,3,8,64,128]{5,4,3,2,1,0:T(8,128)(2,1)} %own_ref.5) | copy-start | bytes 9437188
  2.6 3.1 %copy-start.2 = (bf16[2,256,256]{2,1,0:T(8,128)(2,1)S(1)}, bf16[2,256,256]{2,1,0:T(8,128)(2,1)}, u32[]{:S(2)}) copy-start(bf16[2,256,256]{2,1,0:T(8,128)(2,1)} %constant.14.clone.w_ref) | copy-start | bytes 786436
  3.2 2.5 %collective-permute-start = (bf16[4,1,3,4,64,128]{5,4,3,2,1,0:T(8,128)(2,1)S(1)}, bf16[4,1,3,4,64,128]{5,4,3,2,1,0:T(8,128)(2,1)S(1)}, u32[]{:S(2)}, u32[]{:S(2)}) collective-permute-start(bf16[4,1,3,4,64,128]{5,4,3,2,1,0:T(8,128)(2,1)S(1)} %shard_map.41), channel_id=1, source_target_pairs={{0,1},{1,0},{2,3},{3,2},{4,5},{5,4},{6,7},{7,6},{8,9},{9,8},{10,11... | collective-permute-start | bytes 2359304 | tf_op jit(solution)/shard_map/ppermute | solution.py:342
  5.5 4.6 %collective-permute-start.5 = (bf16[4,1,3,4,64,128]{5,4,3,2,1,0:T(8,128)(2,1)S(1)}, bf16[4,1,3,4,64,128]{5,4,3,2,1,0:T(8,128)(2,1)S(1)}, u32[]{:S(2)}, u32[]{:S(2)}) collective-permute-start(bf16[4,1,3,4,64,128]{5,4,3,2,1,0:T(8,128)(2,1)S(1)} %shard_map.44), channel_id=1, source_target_pairs={{0,1},{1,0},{2,3},{3,2},{4,5},{5,4},{6,7},{7,6},{8,9},{9,8},{10,11... | collective-permute-start | bytes 2359304 | tf_op jit(solution)/shard_map/ppermute | solution.py:342
  7.1 23.3 %collective-permute-start.1 = (bf16[4,272,128]{2,1,0:T(8,128)(2,1)S(1)}, bf16[4,272,128]{2,1,0:T(8,128)(2,1)S(1)}, u32[]{:S(2)}, u32[]{:S(2)}) collective-permute-start(bf16[4,272,128]{2,1,0:T(8,128)(2,1)S(1)} %get-tuple-element.31), channel_id=1, source_target_pairs={{0,2},{2,0},{1,3},{3,1},{4,6},{6,4},{5,7},{7,5},{8,10},{10,8},{9,1... | collective-permute-start | bytes 835592 | tf_op jit(solution)/shard_map/ppermute | solution.py:356
  11.0 9.5 %collective-permute-start.9 = (bf16[2,272,128]{2,1,0:T(8,128)(2,1)S(1)}, bf16[2,272,128]{2,1,0:T(8,128)(2,1)S(1)}, u32[]{:S(2)}, u32[]{:S(2)}) collective-permute-start(bf16[2,272,128]{2,1,0:T(8,128)(2,1)S(1)} %get-tuple-element.43), channel_id=1, source_target_pairs={{0,2},{2,0},{1,3},{3,1},{4,6},{6,4},{5,7},{7,5},{8,10},{10,8},{9,1... | collective-permute-start | bytes 417800 | tf_op jit(solution)/shard_map/ppermute | solution.py:356
  12.4 14.3 %collective-permute-start.6 = (bf16[2,272,128]{2,1,0:T(8,128)(2,1)S(1)}, bf16[2,272,128]{2,1,0:T(8,128)(2,1)S(1)}, u32[]{:S(2)}, u32[]{:S(2)}) collective-permute-start(bf16[2,272,128]{2,1,0:T(8,128)(2,1)S(1)} %get-tuple-element.38), channel_id=1, source_target_pairs={{0,2},{2,0},{1,3},{3,1},{4,6},{6,4},{5,7},{7,5},{8,10},{10,8},{9,1... | collective-permute-start | bytes 417800 | tf_op jit(solution)/shard_map/ppermute | solution.py:356
  21.4 11.8 %collective-permute-start.10 = (bf16[272,128]{1,0:T(8,128)(2,1)S(1)}, bf16[272,128]{1,0:T(8,128)(2,1)S(1)}, u32[]{:S(2)}, u32[]{:S(2)}) collective-permute-start(bf16[272,128]{1,0:T(8,128)(2,1)S(1)} %get-tuple-element.44), channel_id=1, source_target_pairs={{0,24},{4,28},{8,16},{12,20},{16,8},{20,12},{24,0},{28,4},{1,25},{... | collective-permute-start | bytes 208904 | tf_op jit(solution)/shard_map/ppermute | solution.py:366
  25.6 8.9 %collective-permute-start.11 = (bf16[272,128]{1,0:T(8,128)(2,1)S(1)}, bf16[272,128]{1,0:T(8,128)(2,1)S(1)}, u32[]{:S(2)}, u32[]{:S(2)}) collective-permute-start(bf16[272,128]{1,0:T(8,128)(2,1)S(1)} %get-tuple-element.45), channel_id=1, source_target_pairs={{0,28},{4,24},{8,20},{12,16},{16,12},{20,8},{24,4},{28,0},{1,29},{... | collective-permute-start | bytes 208904 | tf_op jit(solution)/shard_map/ppermute | solution.py:366
  27.6 8.3 %collective-permute-start.7 = (bf16[272,128]{1,0:T(8,128)(2,1)S(1)}, bf16[272,128]{1,0:T(8,128)(2,1)S(1)}, u32[]{:S(2)}, u32[]{:S(2)}) collective-permute-start(bf16[272,128]{1,0:T(8,128)(2,1)S(1)} %get-tuple-element.39), channel_id=1, source_target_pairs={{0,16},{4,20},{8,24},{12,28},{16,0},{20,4},{24,8},{28,12},{1,17},{... | collective-permute-start | bytes 208904 | tf_op jit(solution)/shard_map/ppermute | solution.py:366
  28.5 8.1 %collective-permute-start.8 = (bf16[272,128]{1,0:T(8,128)(2,1)S(1)}, bf16[272,128]{1,0:T(8,128)(2,1)S(1)}, u32[]{:S(2)}, u32[]{:S(2)}) collective-permute-start(bf16[272,128]{1,0:T(8,128)(2,1)S(1)} %get-tuple-element.40), channel_id=1, source_target_pairs={{0,20},{4,16},{8,28},{12,24},{16,4},{20,0},{24,12},{28,8},{1,21},{... | collective-permute-start | bytes 208904 | tf_op jit(solution)/shard_map/ppermute | solution.py:366
  31.5 6.0 %collective-permute-start.2 = (bf16[272,128]{1,0:T(8,128)(2,1)S(1)}, bf16[272,128]{1,0:T(8,128)(2,1)S(1)}, u32[]{:S(2)}, u32[]{:S(2)}) collective-permute-start(bf16[272,128]{1,0:T(8,128)(2,1)S(1)} %get-tuple-element.33), channel_id=1, source_target_pairs={{0,4},{4,0},{8,12},{12,8},{16,20},{20,16},{24,28},{28,24},{1,5},{5... | collective-permute-start | bytes 208904 | tf_op jit(solution)/shard_map/ppermute | solution.py:366
  33.2 4.8 %collective-permute-start.3 = (bf16[272,128]{1,0:T(8,128)(2,1)S(1)}, bf16[272,128]{1,0:T(8,128)(2,1)S(1)}, u32[]{:S(2)}, u32[]{:S(2)}) collective-permute-start(bf16[272,128]{1,0:T(8,128)(2,1)S(1)} %get-tuple-element.34), channel_id=1, source_target_pairs={{0,8},{4,12},{8,0},{12,4},{16,24},{20,28},{24,16},{28,20},{1,9},{5... | collective-permute-start | bytes 208904 | tf_op jit(solution)/shard_map/ppermute | solution.py:366
  34.5 5.2 %collective-permute-start.4 = (bf16[272,128]{1,0:T(8,128)(2,1)S(1)}, bf16[272,128]{1,0:T(8,128)(2,1)S(1)}, u32[]{:S(2)}, u32[]{:S(2)}) collective-permute-start(bf16[272,128]{1,0:T(8,128)(2,1)S(1)} %get-tuple-element.35), channel_id=1, source_target_pairs={{0,12},{4,8},{8,4},{12,0},{16,28},{20,24},{24,20},{28,16},{1,13},{... | collective-permute-start | bytes 208904 | tf_op jit(solution)/shard_map/ppermute | solution.py:366
  42.3 7.1 %collective-permute-start.12 = (f32[4,4,32,128]{3,2,1,0:T(8,128)S(1)}, f32[4,4,32,128]{3,2,1,0:T(8,128)S(1)}, u32[]{:S(2)}, u32[]{:S(2)}) collective-permute-start(f32[4,4,32,128]{3,2,1,0:T(8,128)S(1)} %get-tuple-element.55), channel_id=1, source_target_pairs={{0,1},{1,0},{2,3},{3,2},{4,5},{5,4},{6,7},{7,6},{8,9},{9,8},{10,11... | collective-permute-start | bytes 786440 | tf_op jit(solution)/shard_map/ppermute | solution.py:390
  42.4 5.8 %collective-permute-start.13 = (f32[2,32,128]{2,1,0:T(8,128)S(1)}, f32[2,32,128]{2,1,0:T(8,128)S(1)}, u32[]{:S(2)}, u32[]{:S(2)}) collective-permute-start(f32[2,32,128]{2,1,0:T(8,128)S(1)} %shard_map.49), channel_id=1, source_target_pairs={{1,5},{5,9},{9,13},{13,17},{17,21},{21,25},{25,29},{4,0},{8,4},{12... | collective-permute-start | bytes 98312 | tf_op jit(solution)/shard_map/ppermute | solution.py:384
  48.2 1.2 %collective-permute-start.14 = (f32[2,32,128]{2,1,0:T(8,128)S(1)}, f32[2,32,128]{2,1,0:T(8,128)S(1)}, u32[]{:S(2)}, u32[]{:S(2)}) collective-permute-start(f32[2,32,128]{2,1,0:T(8,128)S(1)} %collective-permute-done.13.mine), channel_id=1, source_target_pairs={{0,1},{1,0},{2,3},{3,2},{4,5},{5,4},{6,7},{7,6},{8,9},{9,8},{10,11... | collective-permute-start | bytes 98312 | tf_op jit(solution)/shard_map/ppermute | solution.py:391

commit v3 on v2

--- a/solution.py
+++ b/solution.py
@@ -10,16 +10,16 @@
 from jax.sharding import PartitionSpec as P
 
 
-KNEE = 0.5
-BASE = 2.0**-5
-POWER = 17
+KNEE = 2.0
+BASE = 2.0 ** (-120 / 33)
+POWER = 33
 LOG2E = 1.4426950408889634
 
 
 def encode(d):
     t = d * (BASE / KNEE) + jnp.where(d < 0.0, -BASE, BASE)
     p = t
-    for _ in range(4):
+    for _ in range(5):
         p = p * p
     return (p * t).astype(jnp.bfloat16)
 
@@ -131,7 +131,7 @@
             outs[k][part] = encode(own_ref[k, j] + decode(up_ref[k, part], from_below))
         return carry
 
-    lax.fori_loop(0, 2 * half, body, 0)
+    lax.fori_loop(0, 2 * half, body, 0, unroll=4)
     for k in range(count):
         lo = decode(up_ref[k, main:], from_below)[:group]
         hi = next_ref[k] + decode(down_ref[k, main:], from_above)[group : 2 * group]

time: 51.6 us -> 51.4 us (level)
  no operation moved by 1% of the time
where the time goes in v3:
time: 51.4 us; the launch traced here: 51.2 us
  starting transfers between devices  19.6 us (38%)
  waiting for transfers between devices  16.1 us (31%)
  Pallas kernels  12.7 us (25%)
  local copies, waits for them, and re-layouts  1.9 us (4%)
  between operations  0.74 us (1%)
    pallas_call x11, Pallas kernels, call(): pl.pallas_call(kernel, out_shape=list(outs), grid_spec=pltpu.PrefetchScal...  12.7 us
    ppermute x7, starting transfers between devices, messages(): lax.ppermute(p, 'gx', [(i, i ^ s) for i in range(nx_dev)])  12.5 us
    ppermute x3, waiting for transfers between devices, messages(): below = above = lax.ppermute(up, 'gy', [(0, 1), (1, 0)])  6.45 us
    ppermute x3, starting transfers between devices, messages(): below = above = lax.ppermute(up, 'gy', [(0, 1), (1, 0)])  5.1 us
    ppermute x1, waiting for transfers between devices, stitched(): mine = lax.ppermute(ends, ('gx', 'gz'), above + below)  4.51 us
    ppermute x7, waiting for transfers between devices, messages(): lax.ppermute(p, 'gx', [(i, i ^ s) for i in range(nx_dev)])  3.83 us
    unnamed x6, local copies, waits for them, and re-layouts  1.9 us
    ppermute x1, starting transfers between devices, stitched(): mine = lax.ppermute(ends, ('gx', 'gz'), above + below)  1.29 us
  transfers between devices with their start and end apart: 15, of which 9 were waited for; matrix products, arithmetic and copies ran while one was open for 0% of the time, Pallas kernels for 15%

profile of v3, /device:TPU:0, one launch (start us, length us, event | category | flops | bytes accessed | tf_op | source)
XLA Modules:
  0.0 51.2 jit_solution(6338792793522426467)
XLA Ops:
  0.6 0.1 pad_add_fusion.scal
  0.7 0.0 copy-start
  0.7 1.9 %copy-done = bf16[8,1,3,8,64,128]{5,4,3,2,1,0:T(8,128)(2,1)S(1)} copy-done((bf16[8,1,3,8,64,128]{5,4,3,2,1,0:T(8,128)(2,1)S(1)}, bf16[8,1,3,8,64,128]{5,4,3,2,1,0:T(8,128)(2,1)}, u32[]{:S(2)}) %copy-start) | copy-done | bytes 3145752
  2.6 0.0 copy-start.1
  2.6 0.0 copy-start.2
  2.6 0.6 %shard_map.41 = bf16[4,1,3,4,64,128]{5,4,3,2,1,0:T(8,128)(2,1)S(1)} custom-call(s32[3]{0:T(128)S(1)} %pad_add_fusion.scal, bf16[8,1,3,8,64,128]{5,4,3,2,1,0:T(8,128)(2,1)S(1)} %copy-done), custom_call_target="tpu_custom_call" | custom-call | bytes 3932160 | tf_op jit(solution)/shard_map/pallas_call | solution.py:283
  3.2 0.6 %collective-permute-start = (bf16[4,1,3,4,64,128]{5,4,3,2,1,0:T(8,128)(2,1)S(1)}, bf16[4,1,3,4,64,128]{5,4,3,2,1,0:T(8,128)(2,1)S(1)}, u32[]{:S(2)}, u32[]{:S(2)}) collective-permute-start(bf16[4,1,3,4,64,128]{5,4,3,2,1,0:T(8,128)(2,1)S(1)} %shard_map.41), channel_id=1, source_target_pairs={{0,1},{1,0},{2,3},{3,2},{4,5},{5,4},{6,7},{7,6},{8,9},{9,8},{10,11... | collective-permute-start | bytes 2359304 | tf_op jit(solution)/shard_map/ppermute | solution.py:342
  3.8 1.7 %shard_map.44 = bf16[4,1,3,4,64,128]{5,4,3,2,1,0:T(8,128)(2,1)S(1)} custom-call(s32[3]{0:T(128)S(1)} %pad_add_fusion.scal, bf16[8,1,3,8,64,128]{5,4,3,2,1,0:T(8,128)(2,1)} %own_ref.5), custom_call_target="tpu_custom_call" | custom-call | bytes 3932160 | tf_op jit(solution)/shard_map/pallas_call | solution.py:283
  5.5 0.1 collective-permute-start.5
  5.6 0.1 collective-permute-done.recv_ref
  5.7 0.0 copy-done.1
  5.7 0.0 copy-done.2
  5.7 1.4 %shard_map.42 = (f32[4,8,32,128]{3,2,1,0:T(8,128)S(1)}, bf16[4,272,128]{2,1,0:T(8,128)(2,1)S(1)}, f32[4,8,128]{2,1,0:T(8,128)S(1)}) custom-call(s32[3]{0:T(128)S(1)} %pad_add_fusion.scal, bf16[8,1,3,8,64,128]{5,4,3,2,1,0:T(8,128)(2,1)S(1)} %copy-done.1, bf16[4,1,3,4,64,128]{5,4,3,2,1,0:T(8,128)(2,1)S(1)} %collective-permute-done.recv_ref, ...), custom_call_target="tpu_custom_call" | custom-call | bytes 5013504 | tf_op jit(solution)/shard_map/pallas_call | solution.py:283
  7.1 2.9 %collective-permute-start.1 = (bf16[4,272,128]{2,1,0:T(8,128)(2,1)S(1)}, bf16[4,272,128]{2,1,0:T(8,128)(2,1)S(1)}, u32[]{:S(2)}, u32[]{:S(2)}) collective-permute-start(bf16[4,272,128]{2,1,0:T(8,128)(2,1)S(1)} %get-tuple-element.31), channel_id=1, source_target_pairs={{0,2},{2,0},{1,3},{3,1},{4,6},{6,4},{5,7},{7,5},{8,10},{10,8},{9,1... | collective-permute-start | bytes 835592 | tf_op jit(solution)/shard_map/ppermute | solution.py:356
  10.0 0.0 collective-permute-done.5.recv_ref
  10.1 0.9 %shard_map.47 = (f32[2,8,32,128]{3,2,1,0:T(8,128)S(1)}, bf16[2,272,128]{2,1,0:T(8,128)(2,1)S(1)}, f32[2,8,128]{2,1,0:T(8,128)S(1)}) custom-call(s32[3]{0:T(128)S(1)} %pad_add_fusion.scal, bf16[8,1,3,8,64,128]{5,4,3,2,1,0:T(8,128)(2,1)S(1)} %copy-done.1, bf16[4,1,3,4,64,128]{5,4,3,2,1,0:T(8,128)(2,1)S(1)} %collective-permute-done.5.recv_ref, ...), custom_call_target="tpu_custom_call" | custom-call | bytes 4603904 | tf_op jit(solution)/shard_map/pallas_call | solution.py:283
  11.0 0.5 collective-permute-start.9
  11.5 0.9 %shard_map.45 = (f32[2,8,32,128]{3,2,1,0:T(8,128)S(1)}, bf16[2,272,128]{2,1,0:T(8,128)(2,1)S(1)}, f32[2,8,128]{2,1,0:T(8,128)S(1)}) custom-call(s32[3]{0:T(128)S(1)} %pad_add_fusion.scal, bf16[8,1,3,8,64,128]{5,4,3,2,1,0:T(8,128)(2,1)S(1)} %copy-done.1, bf16[4,1,3,4,64,128]{5,4,3,2,1,0:T(8,128)(2,1)S(1)} %collective-permute-done.5.recv_ref, ...), custom_call_target="tpu_custom_call" | custom-call | bytes 4603904 | tf_op jit(solution)/shard_map/pallas_call | solution.py:283
  12.4 1.7 %collective-permute-start.6 = (bf16[2,272,128]{2,1,0:T(8,128)(2,1)S(1)}, bf16[2,272,128]{2,1,0:T(8,128)(2,1)S(1)}, u32[]{:S(2)}, u32[]{:S(2)}) collective-permute-start(bf16[2,272,128]{2,1,0:T(8,128)(2,1)S(1)} %get-tuple-element.38), channel_id=1, source_target_pairs={{0,2},{2,0},{1,3},{3,1},{4,6},{6,4},{5,7},{7,5},{8,10},{10,8},{9,1... | collective-permute-start | bytes 417800 | tf_op jit(solution)/shard_map/ppermute | solution.py:356
  14.1 6.4 %collective-permute-done.9.up_ref.down_ref = bf16[2,272,128]{2,1,0:T(8,128)(2,1)S(1)} collective-permute-done((bf16[2,272,128]{2,1,0:T(8,128)(2,1)S(1)}, bf16[2,272,128]{2,1,0:T(8,128)(2,1)S(1)}, u32[]{:S(2)}, u32[]{:S(2)}) %collective-permute-start.9) | collective-permute-done | bytes 139296 | tf_op jit(solution)/shard_map/ppermute | solution.py:356
  20.5 0.8 %shard_map.48 = (bf16[272,128]{1,0:T(8,128)(2,1)S(1)}, bf16[272,128]{1,0:T(8,128)(2,1)S(1)}) custom-call(s32[3]{0:T(128)S(1)} %pad_add_fusion.scal, f32[2,8,32,128]{3,2,1,0:T(8,128)S(1)} %get-tuple-element.41.own_ref, f32[2,8,128]{2,1,0:T(8,128)S(1)} %get-tuple-element.42.next_ref, bf16[2,272,128]{2,1,0:T(8,128)(2,1)S(1)} %collective-permute-done.9.up_ref.down_ref, ...), custom_call_target="tpu_custom_call" | custom-call | bytes 688128 | tf_op jit(solution)/shard_map/pallas_call | solution.py:283
  21.3 4.2 %collective-permute-start.10 = (bf16[272,128]{1,0:T(8,128)(2,1)S(1)}, bf16[272,128]{1,0:T(8,128)(2,1)S(1)}, u32[]{:S(2)}, u32[]{:S(2)}) collective-permute-start(bf16[272,128]{1,0:T(8,128)(2,1)S(1)} %get-tuple-element.44), channel_id=1, source_target_pairs={{0,24},{4,28},{8,16},{12,20},{16,8},{20,12},{24,0},{28,4},{1,25},{... | collective-permute-start | bytes 208904 | tf_op jit(solution)/shard_map/ppermute | solution.py:366
  25.5 1.1 %collective-permute-start.11 = (bf16[272,128]{1,0:T(8,128)(2,1)S(1)}, bf16[272,128]{1,0:T(8,128)(2,1)S(1)}, u32[]{:S(2)}, u32[]{:S(2)}) collective-permute-start(bf16[272,128]{1,0:T(8,128)(2,1)S(1)} %get-tuple-element.45), channel_id=1, source_target_pairs={{0,28},{4,24},{8,20},{12,16},{16,12},{20,8},{24,4},{28,0},{1,29},{... | collective-permute-start | bytes 208904 | tf_op jit(solution)/shard_map/ppermute | solution.py:366
  26.6 0.0 collective-permute-done.6.up_ref.down_ref
  26.6 0.8 %shard_map.46 = (bf16[272,128]{1,0:T(8,128)(2,1)S(1)}, bf16[272,128]{1,0:T(8,128)(2,1)S(1)}) custom-call(s32[3]{0:T(128)S(1)} %pad_add_fusion.scal, f32[2,8,32,128]{3,2,1,0:T(8,128)S(1)} %get-tuple-element.36.own_ref, f32[2,8,128]{2,1,0:T(8,128)S(1)} %get-tuple-element.37.next_ref, bf16[2,272,128]{2,1,0:T(8,128)(2,1)S(1)} %collective-permute-done.6.up_ref.down_ref, ...), custom_call_target="tpu_custom_call" | custom-call | bytes 688128 | tf_op jit(solution)/shard_map/pallas_call | solution.py:283
  27.4 0.9 %collective-permute-start.7 = (bf16[272,128]{1,0:T(8,128)(2,1)S(1)}, bf16[272,128]{1,0:T(8,128)(2,1)S(1)}, u32[]{:S(2)}, u32[]{:S(2)}) collective-permute-start(bf16[272,128]{1,0:T(8,128)(2,1)S(1)} %get-tuple-element.39), channel_id=1, source_target_pairs={{0,16},{4,20},{8,24},{12,28},{16,0},{20,4},{24,8},{28,12},{1,17},{... | collective-permute-start | bytes 208904 | tf_op jit(solution)/shard_map/ppermute | solution.py:366
  28.3 2.0 %collective-permute-start.8 = (bf16[272,128]{1,0:T(8,128)(2,1)S(1)}, bf16[272,128]{1,0:T(8,128)(2,1)S(1)}, u32[]{:S(2)}, u32[]{:S(2)}) collective-permute-start(bf16[272,128]{1,0:T(8,128)(2,1)S(1)} %get-tuple-element.40), channel_id=1, source_target_pairs={{0,20},{4,16},{8,28},{12,24},{16,4},{20,0},{24,12},{28,8},{1,21},{... | collective-permute-start | bytes 208904 | tf_op jit(solution)/shard_map/ppermute | solution.py:366
  30.2 0.0 collective-permute-done.1.up_ref.down_ref
  30.2 1.0 %shard_map.43 = (bf16[272,128]{1,0:T(8,128)(2,1)S(1)}, bf16[272,128]{1,0:T(8,128)(2,1)S(1)}, bf16[272,128]{1,0:T(8,128)(2,1)S(1)}, bf16[272,128]{1,0:T(8,128)(2,1)S(1)}) custom-call(s32[3]{0:T(128)S(1)} %pad_add_fusion.scal, f32[4,8,32,128]{3,2,1,0:T(8,128)S(1)} %get-tuple-element.29.own_ref, f32[4,8,128]{2,1,0:T(8,128)S(1)} %get-tuple-element.30.next_ref, ...), custom_call_target="tpu_custom_call" | custom-call | bytes 1376256 | tf_op jit(solution)/shard_map/pallas_call | solution.py:283
  31.2 1.7 %collective-permute-start.2 = (bf16[272,128]{1,0:T(8,128)(2,1)S(1)}, bf16[272,128]{1,0:T(8,128)(2,1)S(1)}, u32[]{:S(2)}, u32[]{:S(2)}) collective-permute-start(bf16[272,128]{1,0:T(8,128)(2,1)S(1)} %get-tuple-element.33), channel_id=1, source_target_pairs={{0,4},{4,0},{8,12},{12,8},{16,20},{20,16},{24,28},{28,24},{1,5},{5... | collective-permute-start | bytes 208904 | tf_op jit(solution)/shard_map/ppermute | solution.py:366
  32.9 0.0 collective-permute-done.10.refs_6_
  32.9 1.3 %collective-permute-start.3 = (bf16[272,128]{1,0:T(8,128)(2,1)S(1)}, bf16[272,128]{1,0:T(8,128)(2,1)S(1)}, u32[]{:S(2)}, u32[]{:S(2)}) collective-permute-start(bf16[272,128]{1,0:T(8,128)(2,1)S(1)} %get-tuple-element.34), channel_id=1, source_target_pairs={{0,8},{4,12},{8,0},{12,4},{16,24},{20,28},{24,16},{28,20},{1,9},{5... | collective-permute-start | bytes 208904 | tf_op jit(solution)/shard_map/ppermute | solution.py:366
  34.2 0.0 collective-permute-done.11.refs_7_
  34.2 1.4 %collective-permute-start.4 = (bf16[272,128]{1,0:T(8,128)(2,1)S(1)}, bf16[272,128]{1,0:T(8,128)(2,1)S(1)}, u32[]{:S(2)}, u32[]{:S(2)}) collective-permute-start(bf16[272,128]{1,0:T(8,128)(2,1)S(1)} %get-tuple-element.35), channel_id=1, source_target_pairs={{0,12},{4,8},{8,4},{12,0},{16,28},{20,24},{24,20},{28,16},{1,13},{... | collective-permute-start | bytes 208904 | tf_op jit(solution)/shard_map/ppermute | solution.py:366
  35.6 0.6 %collective-permute-done.7.refs_4_ = bf16[272,128]{1,0:T(8,128)(2,1)S(1)} collective-permute-done((bf16[272,128]{1,0:T(8,128)(2,1)S(1)}, bf16[272,128]{1,0:T(8,128)(2,1)S(1)}, u32[]{:S(2)}, u32[]{:S(2)}) %collective-permute-start.7) | collective-permute-done | bytes 69664 | tf_op jit(solution)/shard_map/ppermute | solution.py:366
  36.2 0.3 collective-permute-done.8.refs_5_
  36.5 0.7 %collective-permute-done.2.refs_1_ = bf16[272,128]{1,0:T(8,128)(2,1)S(1)} collective-permute-done((bf16[272,128]{1,0:T(8,128)(2,1)S(1)}, bf16[272,128]{1,0:T(8,128)(2,1)S(1)}, u32[]{:S(2)}, u32[]{:S(2)}) %collective-permute-start.2) | collective-permute-done | bytes 69664 | tf_op jit(solution)/shard_map/ppermute | solution.py:366
  37.2 0.7 %collective-permute-done.3.refs_2_ = bf16[272,128]{1,0:T(8,128)(2,1)S(1)} collective-permute-done((bf16[272,128]{1,0:T(8,128)(2,1)S(1)}, bf16[272,128]{1,0:T(8,128)(2,1)S(1)}, u32[]{:S(2)}, u32[]{:S(2)}) %collective-permute-start.3) | collective-permute-done | bytes 69664 | tf_op jit(solution)/shard_map/ppermute | solution.py:366
  37.9 1.6 %collective-permute-done.4.refs_3_ = bf16[272,128]{1,0:T(8,128)(2,1)S(1)} collective-permute-done((bf16[272,128]{1,0:T(8,128)(2,1)S(1)}, bf16[272,128]{1,0:T(8,128)(2,1)S(1)}, u32[]{:S(2)}, u32[]{:S(2)}) %collective-permute-start.4) | collective-permute-done | bytes 69664 | tf_op jit(solution)/shard_map/ppermute | solution.py:366
  39.5 0.8 %shard_map.49 = f32[2,32,128]{2,1,0:T(8,128)S(1)} custom-call(s32[3]{0:T(128)S(1)} %pad_add_fusion.scal, bf16[272,128]{1,0:T(8,128)(2,1)S(1)} %get-tuple-element.46.refs_0_, bf16[272,128]{1,0:T(8,128)(2,1)S(1)} %collective-permute-done.2.refs_1_, bf16[272,128]{1,0:T(8,128)(2,1)S(1)} %collective-permute-done.3.refs_2_, ...), custom_call_target="tpu_custom_call" | custom-call | bytes 589824 | tf_op jit(solution)/shard_map/pallas_call | solution.py:283
  40.2 1.8 %shard_map.50 = (f32[4,4,32,128]{3,2,1,0:T(8,128)S(1)}, f32[4,4,32,128]{3,2,1,0:T(8,128)S(1)}) custom-call(s32[3]{0:T(128)S(1)} %pad_add_fusion.scal, bf16[272,128]{1,0:T(8,128)(2,1)S(1)} %get-tuple-element.46.refs_0_, bf16[272,128]{1,0:T(8,128)(2,1)S(1)} %collective-permute-done.2.refs_1_, bf16[272,128]{1,0:T(8,128)(2,1)S(1)} %collective-permute-done.3.refs_2_, ...), custom_call_target="tpu_custom_call" | custom-call | bytes 1081344 | tf_op jit(solution)/shard_map/pallas_call | solution.py:283
  42.1 0.1 collective-permute-start.12
  42.1 1.3 %collective-permute-start.13 = (f32[2,32,128]{2,1,0:T(8,128)S(1)}, f32[2,32,128]{2,1,0:T(8,128)S(1)}, u32[]{:S(2)}, u32[]{:S(2)}) collective-permute-start(f32[2,32,128]{2,1,0:T(8,128)S(1)} %shard_map.49), channel_id=1, source_target_pairs={{1,5},{5,9},{9,13},{13,17},{17,21},{21,25},{25,29},{4,0},{8,4},{12... | collective-permute-start | bytes 98312 | tf_op jit(solution)/shard_map/ppermute | solution.py:384
  43.4 4.5 %collective-permute-done.13.mine = f32[2,32,128]{2,1,0:T(8,128)S(1)} collective-permute-done((f32[2,32,128]{2,1,0:T(8,128)S(1)}, f32[2,32,128]{2,1,0:T(8,128)S(1)}, u32[]{:S(2)}, u32[]{:S(2)}) %collective-permute-start.13) | collective-permute-done | bytes 32800 | tf_op jit(solution)/shard_map/ppermute | solution.py:384
  47.9 0.0 collective-permute-start.14
  47.9 1.2 %collective-permute-done.14.theirs = f32[2,32,128]{2,1,0:T(8,128)S(1)} collective-permute-done((f32[2,32,128]{2,1,0:T(8,128)S(1)}, f32[2,32,128]{2,1,0:T(8,128)S(1)}, u32[]{:S(2)}, u32[]{:S(2)}) %collective-permute-start.14) | collective-permute-done | bytes 32800 | tf_op jit(solution)/shard_map/ppermute | solution.py:391
  49.1 0.0 collective-permute-done.12.recv
  49.2 2.0 %shard_map.51 = (f32[3,32,32,64]{3,2,1,0:T(8,128)}, f32[32,32,64]{2,1,0:T(8,128)}) custom-call(s32[3]{0:T(128)S(1)} %pad_add_fusion.scal, f32[4,4,32,128]{3,2,1,0:T(8,128)S(1)} %get-tuple-element.54.keep, f32[4,4,32,128]{3,2,1,0:T(8,128)S(1)} %collective-permute-done.12.recv, f32[2,32,128]{2,1,0:T(8,128)S(1)} %collective-permute-done.13.mine, ...), custom_call_target="tpu_custom_call" | custom-call | bytes 1638400 | tf_op jit(solution)/shard_map/pallas_call | solution.py:283
Async XLA Ops:
  0.7 1.9 %copy-start = (bf16[8,1,3,8,64,128]{5,4,3,2,1,0:T(8,128)(2,1)S(1)}, bf16[8,1,3,8,64,128]{5,4,3,2,1,0:T(8,128)(2,1)}, u32[]{:S(2)}) copy-start(bf16[8,1,3,8,64,128]{5,4,3,2,1,0:T(8,128)(2,1)} %own_ref.5) | copy-start | bytes 9437188
  2.6 3.1 %copy-start.1 = (bf16[8,1,3,8,64,128]{5,4,3,2,1,0:T(8,128)(2,1)S(1)}, bf16[8,1,3,8,64,128]{5,4,3,2,1,0:T(8,128)(2,1)}, u32[]{:S(2)}) copy-start(bf16[8,1,3,8,64,128]{5,4,3,2,1,0:T(8,128)(2,1)} %own_ref.5) | copy-start | bytes 9437188
  2.6 3.1 %copy-start.2 = (bf16[2,256,256]{2,1,0:T(8,128)(2,1)S(1)}, bf16[2,256,256]{2,1,0:T(8,128)(2,1)}, u32[]{:S(2)}) copy-start(bf16[2,256,256]{2,1,0:T(8,128)(2,1)} %constant.14.clone.w_ref) | copy-start | bytes 786436
  3.2 2.5 %collective-permute-start = (bf16[4,1,3,4,64,128]{5,4,3,2,1,0:T(8,128)(2,1)S(1)}, bf16[4,1,3,4,64,128]{5,4,3,2,1,0:T(8,128)(2,1)S(1)}, u32[]{:S(2)}, u32[]{:S(2)}) collective-permute-start(bf16[4,1,3,4,64,128]{5,4,3,2,1,0:T(8,128)(2,1)S(1)} %shard_map.41), channel_id=1, source_target_pairs={{0,1},{1,0},{2,3},{3,2},{4,5},{5,4},{6,7},{7,6},{8,9},{9,8},{10,11... | collective-permute-start | bytes 2359304 | tf_op jit(solution)/shard_map/ppermute | solution.py:342
  5.5 4.6 %collective-permute-start.5 = (bf16[4,1,3,4,64,128]{5,4,3,2,1,0:T(8,128)(2,1)S(1)}, bf16[4,1,3,4,64,128]{5,4,3,2,1,0:T(8,128)(2,1)S(1)}, u32[]{:S(2)}, u32[]{:S(2)}) collective-permute-start(bf16[4,1,3,4,64,128]{5,4,3,2,1,0:T(8,128)(2,1)S(1)} %shard_map.44), channel_id=1, source_target_pairs={{0,1},{1,0},{2,3},{3,2},{4,5},{5,4},{6,7},{7,6},{8,9},{9,8},{10,11... | collective-permute-start | bytes 2359304 | tf_op jit(solution)/shard_map/ppermute | solution.py:342
  7.1 23.1 %collective-permute-start.1 = (bf16[4,272,128]{2,1,0:T(8,128)(2,1)S(1)}, bf16[4,272,128]{2,1,0:T(8,128)(2,1)S(1)}, u32[]{:S(2)}, u32[]{:S(2)}) collective-permute-start(bf16[4,272,128]{2,1,0:T(8,128)(2,1)S(1)} %get-tuple-element.31), channel_id=1, source_target_pairs={{0,2},{2,0},{1,3},{3,1},{4,6},{6,4},{5,7},{7,5},{8,10},{10,8},{9,1... | collective-permute-start | bytes 835592 | tf_op jit(solution)/shard_map/ppermute | solution.py:356
  11.0 9.5 %collective-permute-start.9 = (bf16[2,272,128]{2,1,0:T(8,128)(2,1)S(1)}, bf16[2,272,128]{2,1,0:T(8,128)(2,1)S(1)}, u32[]{:S(2)}, u32[]{:S(2)}) collective-permute-start(bf16[2,272,128]{2,1,0:T(8,128)(2,1)S(1)} %get-tuple-element.43), channel_id=1, source_target_pairs={{0,2},{2,0},{1,3},{3,1},{4,6},{6,4},{5,7},{7,5},{8,10},{10,8},{9,1... | collective-permute-start | bytes 417800 | tf_op jit(solution)/shard_map/ppermute | solution.py:356
  12.4 14.2 %collective-permute-start.6 = (bf16[2,272,128]{2,1,0:T(8,128)(2,1)S(1)}, bf16[2,272,128]{2,1,0:T(8,128)(2,1)S(1)}, u32[]{:S(2)}, u32[]{:S(2)}) collective-permute-start(bf16[2,272,128]{2,1,0:T(8,128)(2,1)S(1)} %get-tuple-element.38), channel_id=1, source_target_pairs={{0,2},{2,0},{1,3},{3,1},{4,6},{6,4},{5,7},{7,5},{8,10},{10,8},{9,1... | collective-permute-start | bytes 417800 | tf_op jit(solution)/shard_map/ppermute | solution.py:356
  21.3 11.6 %collective-permute-start.10 = (bf16[272,128]{1,0:T(8,128)(2,1)S(1)}, bf16[272,128]{1,0:T(8,128)(2,1)S(1)}, u32[]{:S(2)}, u32[]{:S(2)}) collective-permute-start(bf16[272,128]{1,0:T(8,128)(2,1)S(1)} %get-tuple-element.44), channel_id=1, source_target_pairs={{0,24},{4,28},{8,16},{12,20},{16,8},{20,12},{24,0},{28,4},{1,25},{... | collective-permute-start | bytes 208904 | tf_op jit(solution)/shard_map/ppermute | solution.py:366
  25.5 8.8 %collective-permute-start.11 = (bf16[272,128]{1,0:T(8,128)(2,1)S(1)}, bf16[272,128]{1,0:T(8,128)(2,1)S(1)}, u32[]{:S(2)}, u32[]{:S(2)}) collective-permute-start(bf16[272,128]{1,0:T(8,128)(2,1)S(1)} %get-tuple-element.45), channel_id=1, source_target_pairs={{0,28},{4,24},{8,20},{12,16},{16,12},{20,8},{24,4},{28,0},{1,29},{... | collective-permute-start | bytes 208904 | tf_op jit(solution)/shard_map/ppermute | solution.py:366
  27.4 8.8 %collective-permute-start.7 = (bf16[272,128]{1,0:T(8,128)(2,1)S(1)}, bf16[272,128]{1,0:T(8,128)(2,1)S(1)}, u32[]{:S(2)}, u32[]{:S(2)}) collective-permute-start(bf16[272,128]{1,0:T(8,128)(2,1)S(1)} %get-tuple-element.39), channel_id=1, source_target_pairs={{0,16},{4,20},{8,24},{12,28},{16,0},{20,4},{24,8},{28,12},{1,17},{... | collective-permute-start | bytes 208904 | tf_op jit(solution)/shard_map/ppermute | solution.py:366
  28.3 8.2 %collective-permute-start.8 = (bf16[272,128]{1,0:T(8,128)(2,1)S(1)}, bf16[272,128]{1,0:T(8,128)(2,1)S(1)}, u32[]{:S(2)}, u32[]{:S(2)}) collective-permute-start(bf16[272,128]{1,0:T(8,128)(2,1)S(1)} %get-tuple-element.40), channel_id=1, source_target_pairs={{0,20},{4,16},{8,28},{12,24},{16,4},{20,0},{24,12},{28,8},{1,21},{... | collective-permute-start | bytes 208904 | tf_op jit(solution)/shard_map/ppermute | solution.py:366
  31.2 6.0 %collective-permute-start.2 = (bf16[272,128]{1,0:T(8,128)(2,1)S(1)}, bf16[272,128]{1,0:T(8,128)(2,1)S(1)}, u32[]{:S(2)}, u32[]{:S(2)}) collective-permute-start(bf16[272,128]{1,0:T(8,128)(2,1)S(1)} %get-tuple-element.33), channel_id=1, source_target_pairs={{0,4},{4,0},{8,12},{12,8},{16,20},{20,16},{24,28},{28,24},{1,5},{5... | collective-permute-start | bytes 208904 | tf_op jit(solution)/shard_map/ppermute | solution.py:366
  32.9 5.0 %collective-permute-start.3 = (bf16[272,128]{1,0:T(8,128)(2,1)S(1)}, bf16[272,128]{1,0:T(8,128)(2,1)S(1)}, u32[]{:S(2)}, u32[]{:S(2)}) collective-permute-start(bf16[272,128]{1,0:T(8,128)(2,1)S(1)} %get-tuple-element.34), channel_id=1, source_target_pairs={{0,8},{4,12},{8,0},{12,4},{16,24},{20,28},{24,16},{28,20},{1,9},{5... | collective-permute-start | bytes 208904 | tf_op jit(solution)/shard_map/ppermute | solution.py:366
  34.2 5.2 %collective-permute-start.4 = (bf16[272,128]{1,0:T(8,128)(2,1)S(1)}, bf16[272,128]{1,0:T(8,128)(2,1)S(1)}, u32[]{:S(2)}, u32[]{:S(2)}) collective-permute-start(bf16[272,128]{1,0:T(8,128)(2,1)S(1)} %get-tuple-element.35), channel_id=1, source_target_pairs={{0,12},{4,8},{8,4},{12,0},{16,28},{20,24},{24,20},{28,16},{1,13},{... | collective-permute-start | bytes 208904 | tf_op jit(solution)/shard_map/ppermute | solution.py:366
  42.1 7.1 %collective-permute-start.12 = (f32[4,4,32,128]{3,2,1,0:T(8,128)S(1)}, f32[4,4,32,128]{3,2,1,0:T(8,128)S(1)}, u32[]{:S(2)}, u32[]{:S(2)}) collective-permute-start(f32[4,4,32,128]{3,2,1,0:T(8,128)S(1)} %get-tuple-element.55), channel_id=1, source_target_pairs={{0,1},{1,0},{2,3},{3,2},{4,5},{5,4},{6,7},{7,6},{8,9},{9,8},{10,11... | collective-permute-start | bytes 786440 | tf_op jit(solution)/shard_map/ppermute | solution.py:390
  42.1 5.8 %collective-permute-start.13 = (f32[2,32,128]{2,1,0:T(8,128)S(1)}, f32[2,32,128]{2,1,0:T(8,128)S(1)}, u32[]{:S(2)}, u32[]{:S(2)}) collective-permute-start(f32[2,32,128]{2,1,0:T(8,128)S(1)} %shard_map.49), channel_id=1, source_target_pairs={{1,5},{5,9},{9,13},{13,17},{17,21},{21,25},{25,29},{4,0},{8,4},{12... | collective-permute-start | bytes 98312 | tf_op jit(solution)/shard_map/ppermute | solution.py:384
  47.9 1.2 %collective-permute-start.14 = (f32[2,32,128]{2,1,0:T(8,128)S(1)}, f32[2,32,128]{2,1,0:T(8,128)S(1)}, u32[]{:S(2)}, u32[]{:S(2)}) collective-permute-start(f32[2,32,128]{2,1,0:T(8,128)S(1)} %collective-permute-done.13.mine), channel_id=1, source_target_pairs={{0,1},{1,0},{2,3},{3,2},{4,5},{5,4},{6,7},{7,6},{8,9},{9,8},{10,11... | collective-permute-start | bytes 98312 | tf_op jit(solution)/shard_map/ppermute | solution.py:391

commit v4 on v3

--- a/solution.py
+++ b/solution.py
@@ -59,11 +59,16 @@
     return np.stack([both, np.roll(both, count * length // 2, 0)])
 
 
+def place():
+    return tuple(lax.axis_index(name) for name in ("gx", "gy", "gz"))
+
+
 def index(shape, axis):
     return lax.broadcasted_iota(jnp.int32, shape, axis)
 
 
-def pick_kernel(dims, scal, patches, out, sem):
+def pick_kernel(dims, patches, out, sem):
+    scal = place()
     count, half = dims["count"], dims["half"]
     start = dims["base"](scal[0], scal[2])
     rows = pl.ds((1 - scal[2]) * half, half)
@@ -72,7 +77,8 @@
     copy.wait()
 
 
-def fold_kernel(dims, scal, own_ref, recv_ref, w_ref, own_out, up_out, next_out, ny, edge):
+def fold_kernel(dims, own_ref, recv_ref, w_ref, own_out, up_out, next_out, ny, edge):
+    scal = place()
     length, half, stride, first = dims["length"], dims["half"], dims["stride"], dims["first"]
     g, row, core = scal[0], scal[1], scal[2]
     begin = (g * 2 + core) * half
@@ -116,7 +122,8 @@
     lax.fori_loop(0, dims["count"], body, 0, unroll=2)
 
 
-def join_kernel(dims, scal, own_ref, next_ref, up_ref, down_ref, *refs):
+def join_kernel(dims, own_ref, next_ref, up_ref, down_ref, *refs):
+    scal = place()
     half, stride, count, edge_rows = dims["half"], dims["stride"], dims["count"], dims["edge"]
     far = refs[:-count]
     outs = refs[len(far) : len(far) + count]
@@ -189,7 +196,8 @@
     )
 
 
-def edge_kernel(dims, scal, *refs):
+def edge_kernel(dims, *refs):
+    scal = place()
     half, slabs = dims["half"], dims["slabs"]
     codes, ends, pad = refs[: 2 * slabs], refs[-2], refs[-1]
     g, core = scal[0], scal[2]
@@ -206,7 +214,8 @@
             ends[1] = z1
 
 
-def smooth_kernel(dims, scal, *refs):
+def smooth_kernel(dims, *refs):
+    scal = place()
     half, slabs = dims["half"], dims["slabs"]
     codes, keep, send, pad = refs[: 2 * slabs], refs[-3], refs[-2], refs[-1]
     g, core = scal[0], scal[2]
@@ -221,7 +230,8 @@
             send[t, u] = jnp.where(low, z1, z0)
 
 
-def finish_kernel(dims, scal, keep, recv, mine, theirs, smooth, confidence):
+def finish_kernel(dims, keep, recv, mine, theirs, smooth, confidence):
+    scal = place()
     half, stride, slabs, depth = dims["half"], dims["stride"], dims["slabs"], dims["depth"]
     step = dims["step"]
     g, row, core = scal[0], scal[1], scal[2]
@@ -276,23 +286,20 @@
     return jax.ShapeDtypeStruct(shape, dtype)
 
 
-def call(kernel, scal, args, outs, in_specs=None, out_specs=None, grid=(1,), scratch=(),
+def call(kernel, args, outs, in_specs=None, out_specs=None, grid=(1,), scratch=(),
          mib=4, flops=0):
     args = list(args)
     size = sum(math.prod(a.shape) * a.dtype.itemsize for a in args + list(outs))
     return pl.pallas_call(
         kernel,
         out_shape=list(outs),
-        grid_spec=pltpu.PrefetchScalarGridSpec(
-            num_scalar_prefetch=1,
-            grid=grid,
-            in_specs=in_specs or [whole(a.shape) for a in args],
-            out_specs=out_specs or [whole(o.shape) for o in outs],
-            scratch_shapes=list(scratch),
-        ),
+        grid=grid,
+        in_specs=in_specs or [whole(a.shape) for a in args],
+        out_specs=out_specs or [whole(o.shape) for o in outs],
+        scratch_shapes=list(scratch),
         compiler_params=pltpu.CompilerParams(vmem_limit_bytes=int(mib * 2**20)),
         cost_estimate=pl.CostEstimate(flops=flops, bytes_accessed=size, transcendentals=0),
-    )(scal, *args)
+    )(*args)
 
 
 def stitched(patches):
@@ -308,8 +315,6 @@
     edge, edge_y = (-(-n * 2 * half // 16) * 16 for n in (2, 2 + far))
     main = 2 * half * stride
     rows, rows_up = main + edge, main + edge_y
-    g, row, core = (lax.axis_index(n) for n in ("gx", "gy", "gz"))
-    scal = jnp.stack([g, row, core]).astype(jnp.int32)
     dims = dict(
         length=length, half=half, stride=stride, slabs=slabs, rows=rows, edge=edge, far=far,
         rows_y=ny_dev, depth=depth, extent_x=positions * stride,
@@ -332,7 +337,7 @@
 
         shape = (slabs, 1, 3, half, length, 128)
         (other,) = call(
-            functools.partial(pick_kernel, dict(dims, count=slabs, base=base)), scal,
+            functools.partial(pick_kernel, dict(dims, count=slabs, base=base)),
             [pltpu.with_memory_space_constraint(patches, pltpu.HBM) if first else patches],
             [pltpu.VMEM(shape, jnp.bfloat16)],
             in_specs=[pl.BlockSpec(memory_space=pl.ANY)],
@@ -344,7 +349,7 @@
     def messages(first, count, recv, base):
         d = dict(dims, first=first, count=count, base=base)
         own, up, ahead = call(
-            functools.partial(fold_kernel, d), scal, [patches, recv, weights],
+            functools.partial(fold_kernel, d), [patches, recv, weights],
             [
                 like((count, 2 * half, stride, 128)),
                 like((count, rows_up, 128), jnp.bfloat16),
@@ -358,7 +363,7 @@
             below, above = ship(up, "gy", 1), ship(up, "gy", -1)
         beyond = [ship(up, "gy", 2)] * far
         parts = call(
-            functools.partial(join_kernel, d), scal,
+            functools.partial(join_kernel, d),
             [own, ahead, below, above] + beyond,
             [like((rows, 128), jnp.bfloat16)] * count,
         )
@@ -371,12 +376,13 @@
     recv_near = swapped(0)
     first = messages(slabs, slabs // 2, *recv_far)
     second = messages(slabs + slabs // 2, slabs // 2, *recv_far)
-    third = messages(0, slabs, *recv_near)
+    third = messages(1, slabs - 1, *recv_near)
+    third = messages(0, 1, *recv_near) + third
     codes = third + first + second
 
     half_rows = (slabs, half, stride, 128)
     (ends,) = call(
-        functools.partial(edge_kernel, dims), scal, codes, [like((2, stride, 128))],
+        functools.partial(edge_kernel, dims), codes, [like((2, stride, 128))],
         scratch=[vmem(half, 2, stride + 16, 128)],
     )
     above = [(2 * i + 1, 2 * i + 3) for i in range(nx_dev - 1)]
@@ -384,7 +390,7 @@
     mine = lax.ppermute(ends, ("gx", "gz"), above + below)
     codes, _ = lax.optimization_barrier((codes, ends))
     keep, send = call(
-        functools.partial(smooth_kernel, dims), scal, codes, [like(half_rows)] * 2,
+        functools.partial(smooth_kernel, dims), codes, [like(half_rows)] * 2,
         scratch=[vmem(slabs, half, 2, stride + 16, 128)],
     )
     recv = lax.ppermute(send, "gz", [(0, 1), (1, 0)])
@@ -393,12 +399,12 @@
     step = slabs // 2
     return tuple(
         call(
-            functools.partial(finish_kernel, dict(dims, step=step)), scal,
+            functools.partial(finish_kernel, dict(dims, step=step)),
             [keep, recv, mine, theirs],
             [like((3, stride, stride, depth)), like((stride, stride, depth))],
             out_specs=[
-                pl.BlockSpec((3, 2 * half * step, stride, depth), lambda i, s: (0, i, 0, 0)),
-                pl.BlockSpec((2 * half * step, stride, depth), lambda i, s: (i, 0, 0)),
+                pl.BlockSpec((3, 2 * half * step, stride, depth), lambda i: (0, i, 0, 0)),
+                pl.BlockSpec((2 * half * step, stride, depth), lambda i: (i, 0, 0)),
             ],
             grid=(slabs // step,),
             mib=8,

time: 51.4 us -> 45.4 us (0.88)
  the two profiles are of different devices: /device:TPU:0 before, /device:TPU:18 now
where the time goes in v4:
time: 45.4 us; the launch traced here: 44.6 us
  waiting for transfers between devices  18.2 us (40%)
  starting transfers between devices  16.9 us (37%)
  Pallas kernels  6.82 us (15%)
  local copies, waits for them, and re-layouts  1.89 us (4%)
  between operations  0.77 us (2%)
    ppermute x7, starting transfers between devices, messages(): lax.ppermute(p, 'gx', [(i, i ^ s) for i in range(nx_dev)])  7.85 us
    ppermute x7, waiting for transfers between devices, messages(): lax.ppermute(p, 'gx', [(i, i ^ s) for i in range(nx_dev)])  7.64 us
    pallas_call x13, Pallas kernels, call(): pl.pallas_call(kernel, out_shape=list(outs), grid=grid, in_specs=in_specs...  6.82 us
    ppermute x4, waiting for transfers between devices, messages(): below = above = lax.ppermute(up, 'gy', [(0, 1), (1, 0)])  5.83 us
    ppermute x4, starting transfers between devices, messages(): below = above = lax.ppermute(up, 'gy', [(0, 1), (1, 0)])  4.77 us
    ppermute x1, starting transfers between devices, stitched(): mine = lax.ppermute(ends, ('gx', 'gz'), above + below)  3.55 us
    ppermute x1, waiting for transfers between devices, stitched(): mine = lax.ppermute(ends, ('gx', 'gz'), above + below)  3.15 us
    unnamed x6, local copies, waits for them, and re-layouts  1.89 us
  transfers between devices with their start and end apart: 16, of which 10 were waited for; matrix products, arithmetic and copies ran while one was open for 0% of the time, Pallas kernels for 8%

profile of v4, /device:TPU:18, one launch (start us, length us, event | category | flops | bytes accessed | tf_op | source)
XLA Modules:
  0.0 44.6 jit_solution(749530500305896345)
XLA Ops:
  0.6 0.0 copy-start
  0.6 1.9 %copy-done = bf16[8,1,3,8,64,128]{5,4,3,2,1,0:T(8,128)(2,1)S(1)} copy-done((bf16[8,1,3,8,64,128]{5,4,3,2,1,0:T(8,128)(2,1)S(1)}, bf16[8,1,3,8,64,128]{5,4,3,2,1,0:T(8,128)(2,1)}, u32[]{:S(2)}) %copy-start) | copy-done | bytes 3145752
  2.5 0.1 shard_map.41
  2.6 0.1 collective-permute-start
  2.7 1.3 %shard_map.46 = bf16[4,1,3,4,64,128]{5,4,3,2,1,0:T(8,128)(2,1)S(1)} custom-call(bf16[8,1,3,8,64,128]{5,4,3,2,1,0:T(8,128)(2,1)} %own_ref.7), custom_call_target="tpu_custom_call" | custom-call | bytes 3932160 | tf_op jit(solution)/shard_map/pallas_call | solution.py:293
  4.0 0.6 %collective-permute-start.6 = (bf16[4,1,3,4,64,128]{5,4,3,2,1,0:T(8,128)(2,1)S(1)}, bf16[4,1,3,4,64,128]{5,4,3,2,1,0:T(8,128)(2,1)S(1)}, u32[]{:S(2)}, u32[]{:S(2)}) collective-permute-start(bf16[4,1,3,4,64,128]{5,4,3,2,1,0:T(8,128)(2,1)S(1)} %shard_map.46), channel_id=1, source_target_pairs={{0,1},{1,0},{2,3},{3,2},{4,5},{5,4},{6,7},{7,6},{8,9},{9,8},{10,11... | collective-permute-start | bytes 2359304 | tf_op jit(solution)/shard_map/ppermute | solution.py:347
  4.6 0.4 collective-permute-done.recv_ref
  5.0 0.0 copy-done.2
  5.0 0.5 %shard_map.44 = (f32[3,8,32,128]{3,2,1,0:T(8,128)S(1)}, bf16[3,272,128]{2,1,0:T(8,128)(2,1)S(1)}, f32[3,8,128]{2,1,0:T(8,128)S(1)}) custom-call(bf16[8,1,3,8,64,128]{5,4,3,2,1,0:T(8,128)(2,1)S(1)} %copy-done.1, bf16[4,1,3,4,64,128]{5,4,3,2,1,0:T(8,128)(2,1)S(1)} %collective-permute-done.recv_ref, bf16[2,256,256]{2,1,0:T(8,128)(2,1)S(1)} %copy-done.2), custom_call_target="tpu_custom_call" | custom-call | bytes 4808704 | tf_op jit(solution)/shard_map/pallas_call | solution.py:293
  5.5 1.6 %collective-permute-start.2 = (bf16[3,272,128]{2,1,0:T(8,128)(2,1)S(1)}, bf16[3,272,128]{2,1,0:T(8,128)(2,1)S(1)}, u32[]{:S(2)}, u32[]{:S(2)}) collective-permute-start(bf16[3,272,128]{2,1,0:T(8,128)(2,1)S(1)} %get-tuple-element.36), channel_id=1, source_target_pairs={{0,2},{2,0},{1,3},{3,1},{4,6},{6,4},{5,7},{7,5},{8,10},{10,8},{9,1... | collective-permute-start | bytes 626696 | tf_op jit(solution)/shard_map/ppermute | solution.py:361
  7.1 0.0 collective-permute-done.6.recv_ref
  7.1 0.4 shard_map.49
  7.5 1.0 %collective-permute-start.10 = (bf16[2,272,128]{2,1,0:T(8,128)(2,1)S(1)}, bf16[2,272,128]{2,1,0:T(8,128)(2,1)S(1)}, u32[]{:S(2)}, u32[]{:S(2)}) collective-permute-start(bf16[2,272,128]{2,1,0:T(8,128)(2,1)S(1)} %get-tuple-element.47), channel_id=1, source_target_pairs={{0,2},{2,0},{1,3},{3,1},{4,6},{6,4},{5,7},{7,5},{8,10},{10,8},{9,1... | collective-permute-start | bytes 417800 | tf_op jit(solution)/shard_map/ppermute | solution.py:361
  8.5 0.4 shard_map.47
  8.9 1.1 %collective-permute-start.7 = (bf16[2,272,128]{2,1,0:T(8,128)(2,1)S(1)}, bf16[2,272,128]{2,1,0:T(8,128)(2,1)S(1)}, u32[]{:S(2)}, u32[]{:S(2)}) collective-permute-start(bf16[2,272,128]{2,1,0:T(8,128)(2,1)S(1)} %get-tuple-element.42), channel_id=1, source_target_pairs={{0,2},{2,0},{1,3},{3,1},{4,6},{6,4},{5,7},{7,5},{8,10},{10,8},{9,1... | collective-permute-start | bytes 417800 | tf_op jit(solution)/shard_map/ppermute | solution.py:361
  10.0 0.3 shard_map.42
  10.3 1.0 %collective-permute-start.1 = (bf16[1,272,128]{2,1,0:T(8,128)(2,1)S(1)}, bf16[1,272,128]{2,1,0:T(8,128)(2,1)S(1)}, u32[]{:S(2)}, u32[]{:S(2)}) collective-permute-start(bf16[1,272,128]{2,1,0:T(8,128)(2,1)S(1)} %get-tuple-element.33), channel_id=1, source_target_pairs={{0,2},{2,0},{1,3},{3,1},{4,6},{6,4},{5,7},{7,5},{8,10},{10,8},{9,1... | collective-permute-start | bytes 208904 | tf_op jit(solution)/shard_map/ppermute | solution.py:361
  11.3 5.2 %collective-permute-done.10.up_ref.down_ref = bf16[2,272,128]{2,1,0:T(8,128)(2,1)S(1)} collective-permute-done((bf16[2,272,128]{2,1,0:T(8,128)(2,1)S(1)}, bf16[2,272,128]{2,1,0:T(8,128)(2,1)S(1)}, u32[]{:S(2)}, u32[]{:S(2)}) %collective-permute-start.10) | collective-permute-done | bytes 139296 | tf_op jit(solution)/shard_map/ppermute | solution.py:361
  16.6 0.2 shard_map.50
  16.8 0.5 %collective-permute-start.11 = (bf16[272,128]{1,0:T(8,128)(2,1)S(1)}, bf16[272,128]{1,0:T(8,128)(2,1)S(1)}, u32[]{:S(2)}, u32[]{:S(2)}) collective-permute-start(bf16[272,128]{1,0:T(8,128)(2,1)S(1)} %get-tuple-element.48), channel_id=1, source_target_pairs={{0,24},{4,28},{8,16},{12,20},{16,8},{20,12},{24,0},{28,4},{1,25},{... | collective-permute-start | bytes 208904 | tf_op jit(solution)/shard_map/ppermute | solution.py:371
  17.3 1.5 %collective-permute-start.12 = (bf16[272,128]{1,0:T(8,128)(2,1)S(1)}, bf16[272,128]{1,0:T(8,128)(2,1)S(1)}, u32[]{:S(2)}, u32[]{:S(2)}) collective-permute-start(bf16[272,128]{1,0:T(8,128)(2,1)S(1)} %get-tuple-element.49), channel_id=1, source_target_pairs={{0,28},{4,24},{8,20},{12,16},{16,12},{20,8},{24,4},{28,0},{1,29},{... | collective-permute-start | bytes 208904 | tf_op jit(solution)/shard_map/ppermute | solution.py:371
  18.8 0.6 %collective-permute-done.7.up_ref.down_ref = bf16[2,272,128]{2,1,0:T(8,128)(2,1)S(1)} collective-permute-done((bf16[2,272,128]{2,1,0:T(8,128)(2,1)S(1)}, bf16[2,272,128]{2,1,0:T(8,128)(2,1)S(1)}, u32[]{:S(2)}, u32[]{:S(2)}) %collective-permute-start.7) | collective-permute-done | bytes 139296 | tf_op jit(solution)/shard_map/ppermute | solution.py:361
  19.5 0.2 shard_map.48
  19.7 1.4 %collective-permute-start.8 = (bf16[272,128]{1,0:T(8,128)(2,1)S(1)}, bf16[272,128]{1,0:T(8,128)(2,1)S(1)}, u32[]{:S(2)}, u32[]{:S(2)}) collective-permute-start(bf16[272,128]{1,0:T(8,128)(2,1)S(1)} %get-tuple-element.43), channel_id=1, source_target_pairs={{0,16},{4,20},{8,24},{12,28},{16,0},{20,4},{24,8},{28,12},{1,17},{... | collective-permute-start | bytes 208904 | tf_op jit(solution)/shard_map/ppermute | solution.py:371
  21.1 0.0 collective-permute-done.2.up_ref.down_ref
  21.1 1.9 %collective-permute-start.9 = (bf16[272,128]{1,0:T(8,128)(2,1)S(1)}, bf16[272,128]{1,0:T(8,128)(2,1)S(1)}, u32[]{:S(2)}, u32[]{:S(2)}) collective-permute-start(bf16[272,128]{1,0:T(8,128)(2,1)S(1)} %get-tuple-element.44), channel_id=1, source_target_pairs={{0,20},{4,16},{8,28},{12,24},{16,4},{20,0},{24,12},{28,8},{1,21},{... | collective-permute-start | bytes 208904 | tf_op jit(solution)/shard_map/ppermute | solution.py:371
  23.0 0.3 shard_map.45
  23.3 0.0 collective-permute-done.1.up_ref.down_ref
  23.3 1.2 %collective-permute-start.3 = (bf16[272,128]{1,0:T(8,128)(2,1)S(1)}, bf16[272,128]{1,0:T(8,128)(2,1)S(1)}, u32[]{:S(2)}, u32[]{:S(2)}) collective-permute-start(bf16[272,128]{1,0:T(8,128)(2,1)S(1)} %get-tuple-element.37), channel_id=1, source_target_pairs={{0,4},{4,0},{8,12},{12,8},{16,20},{20,16},{24,28},{28,24},{1,5},{5... | collective-permute-start | bytes 208904 | tf_op jit(solution)/shard_map/ppermute | solution.py:371
  24.5 1.5 %collective-permute-done.11.refs_6_ = bf16[272,128]{1,0:T(8,128)(2,1)S(1)} collective-permute-done((bf16[272,128]{1,0:T(8,128)(2,1)S(1)}, bf16[272,128]{1,0:T(8,128)(2,1)S(1)}, u32[]{:S(2)}, u32[]{:S(2)}) %collective-permute-start.11) | collective-permute-done | bytes 69664 | tf_op jit(solution)/shard_map/ppermute | solution.py:371
  26.0 1.3 %collective-permute-start.4 = (bf16[272,128]{1,0:T(8,128)(2,1)S(1)}, bf16[272,128]{1,0:T(8,128)(2,1)S(1)}, u32[]{:S(2)}, u32[]{:S(2)}) collective-permute-start(bf16[272,128]{1,0:T(8,128)(2,1)S(1)} %get-tuple-element.38), channel_id=1, source_target_pairs={{0,8},{4,12},{8,0},{12,4},{16,24},{20,28},{24,16},{28,20},{1,9},{5... | collective-permute-start | bytes 208904 | tf_op jit(solution)/shard_map/ppermute | solution.py:371
  27.3 1.1 %collective-permute-done.12.refs_7_ = bf16[272,128]{1,0:T(8,128)(2,1)S(1)} collective-permute-done((bf16[272,128]{1,0:T(8,128)(2,1)S(1)}, bf16[272,128]{1,0:T(8,128)(2,1)S(1)}, u32[]{:S(2)}, u32[]{:S(2)}) %collective-permute-start.12) | collective-permute-done | bytes 69664 | tf_op jit(solution)/shard_map/ppermute | solution.py:371
  28.4 0.0 collective-permute-start.5
  28.4 0.1 shard_map.43.refs_0_
  28.5 0.0 collective-permute-done.8.refs_4_
  28.5 0.0 collective-permute-done.9.refs_5_
  28.6 0.7 %collective-permute-done.3.refs_1_ = bf16[272,128]{1,0:T(8,128)(2,1)S(1)} collective-permute-done((bf16[272,128]{1,0:T(8,128)(2,1)S(1)}, bf16[272,128]{1,0:T(8,128)(2,1)S(1)}, u32[]{:S(2)}, u32[]{:S(2)}) %collective-permute-start.3) | collective-permute-done | bytes 69664 | tf_op jit(solution)/shard_map/ppermute | solution.py:371
  29.3 1.0 %collective-permute-done.4.refs_2_ = bf16[272,128]{1,0:T(8,128)(2,1)S(1)} collective-permute-done((bf16[272,128]{1,0:T(8,128)(2,1)S(1)}, bf16[272,128]{1,0:T(8,128)(2,1)S(1)}, u32[]{:S(2)}, u32[]{:S(2)}) %collective-permute-start.4) | collective-permute-done | bytes 69664 | tf_op jit(solution)/shard_map/ppermute | solution.py:371
  30.3 3.3 %collective-permute-done.5.refs_3_ = bf16[272,128]{1,0:T(8,128)(2,1)S(1)} collective-permute-done((bf16[272,128]{1,0:T(8,128)(2,1)S(1)}, bf16[272,128]{1,0:T(8,128)(2,1)S(1)}, u32[]{:S(2)}, u32[]{:S(2)}) %collective-permute-start.5) | collective-permute-done | bytes 69664 | tf_op jit(solution)/shard_map/ppermute | solution.py:371
  33.6 0.2 shard_map.51
  33.8 1.3 %shard_map.52 = (f32[4,4,32,128]{3,2,1,0:T(8,128)S(1)}, f32[4,4,32,128]{3,2,1,0:T(8,128)S(1)}) custom-call(bf16[272,128]{1,0:T(8,128)(2,1)S(1)} %shard_map.43.refs_0_, bf16[272,128]{1,0:T(8,128)(2,1)S(1)} %collective-permute-done.3.refs_1_, bf16[272,128]{1,0:T(8,128)(2,1)S(1)} %collective-permute-done.4.refs_2_, ...), custom_call_target="tpu_custom_call" | custom-call | bytes 1081344 | tf_op jit(solution)/shard_map/pallas_call | solution.py:293
  35.1 0.1 collective-permute-start.13
  35.2 3.5 %collective-permute-start.14 = (f32[2,32,128]{2,1,0:T(8,128)S(1)}, f32[2,32,128]{2,1,0:T(8,128)S(1)}, u32[]{:S(2)}, u32[]{:S(2)}) collective-permute-start(f32[2,32,128]{2,1,0:T(8,128)S(1)} %shard_map.51), channel_id=1, source_target_pairs={{1,5},{5,9},{9,13},{13,17},{17,21},{21,25},{25,29},{4,0},{8,4},{12... | collective-permute-start | bytes 98312 | tf_op jit(solution)/shard_map/ppermute | solution.py:390
  38.7 3.1 %collective-permute-done.14.mine = f32[2,32,128]{2,1,0:T(8,128)S(1)} collective-permute-done((f32[2,32,128]{2,1,0:T(8,128)S(1)}, f32[2,32,128]{2,1,0:T(8,128)S(1)}, u32[]{:S(2)}, u32[]{:S(2)}) %collective-permute-start.14) | collective-permute-done | bytes 32800 | tf_op jit(solution)/shard_map/ppermute | solution.py:390
  41.9 0.0 collective-permute-start.15
  41.9 1.2 %collective-permute-done.15.theirs = f32[2,32,128]{2,1,0:T(8,128)S(1)} collective-permute-done((f32[2,32,128]{2,1,0:T(8,128)S(1)}, f32[2,32,128]{2,1,0:T(8,128)S(1)}, u32[]{:S(2)}, u32[]{:S(2)}) %collective-permute-start.15) | collective-permute-done | bytes 32800 | tf_op jit(solution)/shard_map/ppermute | solution.py:397
  43.1 0.0 collective-permute-done.13.recv
  43.1 1.5 %shard_map.53 = (f32[3,32,32,64]{3,2,1,0:T(8,128)}, f32[32,32,64]{2,1,0:T(8,128)}) custom-call(f32[4,4,32,128]{3,2,1,0:T(8,128)S(1)} %get-tuple-element.58.keep, f32[4,4,32,128]{3,2,1,0:T(8,128)S(1)} %collective-permute-done.13.recv, f32[2,32,128]{2,1,0:T(8,128)S(1)} %collective-permute-done.14.mine, f32[2,32,128]{2,1,0:T(8,128)S(1)} %collective-permute-done.15.theirs), custom_call_target="tpu_custom_call" | custom-call | bytes 1638400 | tf_op jit(solution)/shard_map/pallas_call | solution.py:293
  (3 shorter events, 0.0 us)
Async XLA Ops:
  0.6 1.9 %copy-start = (bf16[8,1,3,8,64,128]{5,4,3,2,1,0:T(8,128)(2,1)S(1)}, bf16[8,1,3,8,64,128]{5,4,3,2,1,0:T(8,128)(2,1)}, u32[]{:S(2)}) copy-start(bf16[8,1,3,8,64,128]{5,4,3,2,1,0:T(8,128)(2,1)} %own_ref.7) | copy-start | bytes 9437188
  2.5 2.4 %copy-start.1 = (bf16[8,1,3,8,64,128]{5,4,3,2,1,0:T(8,128)(2,1)S(1)}, bf16[8,1,3,8,64,128]{5,4,3,2,1,0:T(8,128)(2,1)}, u32[]{:S(2)}) copy-start(bf16[8,1,3,8,64,128]{5,4,3,2,1,0:T(8,128)(2,1)} %own_ref.7) | copy-start | bytes 9437188
  2.5 2.4 %copy-start.2 = (bf16[2,256,256]{2,1,0:T(8,128)(2,1)S(1)}, bf16[2,256,256]{2,1,0:T(8,128)(2,1)}, u32[]{:S(2)}) copy-start(bf16[2,256,256]{2,1,0:T(8,128)(2,1)} %constant.2.clone.w_ref) | copy-start | bytes 786436
  2.6 2.4 %collective-permute-start = (bf16[4,1,3,4,64,128]{5,4,3,2,1,0:T(8,128)(2,1)S(1)}, bf16[4,1,3,4,64,128]{5,4,3,2,1,0:T(8,128)(2,1)S(1)}, u32[]{:S(2)}, u32[]{:S(2)}) collective-permute-start(bf16[4,1,3,4,64,128]{5,4,3,2,1,0:T(8,128)(2,1)S(1)} %shard_map.41), channel_id=1, source_target_pairs={{0,1},{1,0},{2,3},{3,2},{4,5},{5,4},{6,7},{7,6},{8,9},{9,8},{10,11... | collective-permute-start | bytes 2359304 | tf_op jit(solution)/shard_map/ppermute | solution.py:347
  4.0 3.1 %collective-permute-start.6 = (bf16[4,1,3,4,64,128]{5,4,3,2,1,0:T(8,128)(2,1)S(1)}, bf16[4,1,3,4,64,128]{5,4,3,2,1,0:T(8,128)(2,1)S(1)}, u32[]{:S(2)}, u32[]{:S(2)}) collective-permute-start(bf16[4,1,3,4,64,128]{5,4,3,2,1,0:T(8,128)(2,1)S(1)} %shard_map.46), channel_id=1, source_target_pairs={{0,1},{1,0},{2,3},{3,2},{4,5},{5,4},{6,7},{7,6},{8,9},{9,8},{10,11... | collective-permute-start | bytes 2359304 | tf_op jit(solution)/shard_map/ppermute | solution.py:347
  5.5 15.7 %collective-permute-start.2 = (bf16[3,272,128]{2,1,0:T(8,128)(2,1)S(1)}, bf16[3,272,128]{2,1,0:T(8,128)(2,1)S(1)}, u32[]{:S(2)}, u32[]{:S(2)}) collective-permute-start(bf16[3,272,128]{2,1,0:T(8,128)(2,1)S(1)} %get-tuple-element.36), channel_id=1, source_target_pairs={{0,2},{2,0},{1,3},{3,1},{4,6},{6,4},{5,7},{7,5},{8,10},{10,8},{9,1... | collective-permute-start | bytes 626696 | tf_op jit(solution)/shard_map/ppermute | solution.py:361
  7.5 9.1 %collective-permute-start.10 = (bf16[2,272,128]{2,1,0:T(8,128)(2,1)S(1)}, bf16[2,272,128]{2,1,0:T(8,128)(2,1)S(1)}, u32[]{:S(2)}, u32[]{:S(2)}) collective-permute-start(bf16[2,272,128]{2,1,0:T(8,128)(2,1)S(1)} %get-tuple-element.47), channel_id=1, source_target_pairs={{0,2},{2,0},{1,3},{3,1},{4,6},{6,4},{5,7},{7,5},{8,10},{10,8},{9,1... | collective-permute-start | bytes 417800 | tf_op jit(solution)/shard_map/ppermute | solution.py:361
  8.9 10.6 %collective-permute-start.7 = (bf16[2,272,128]{2,1,0:T(8,128)(2,1)S(1)}, bf16[2,272,128]{2,1,0:T(8,128)(2,1)S(1)}, u32[]{:S(2)}, u32[]{:S(2)}) collective-permute-start(bf16[2,272,128]{2,1,0:T(8,128)(2,1)S(1)} %get-tuple-element.42), channel_id=1, source_target_pairs={{0,2},{2,0},{1,3},{3,1},{4,6},{6,4},{5,7},{7,5},{8,10},{10,8},{9,1... | collective-permute-start | bytes 417800 | tf_op jit(solution)/shard_map/ppermute | solution.py:361
  10.3 13.0 %collective-permute-start.1 = (bf16[1,272,128]{2,1,0:T(8,128)(2,1)S(1)}, bf16[1,272,128]{2,1,0:T(8,128)(2,1)S(1)}, u32[]{:S(2)}, u32[]{:S(2)}) collective-permute-start(bf16[1,272,128]{2,1,0:T(8,128)(2,1)S(1)} %get-tuple-element.33), channel_id=1, source_target_pairs={{0,2},{2,0},{1,3},{3,1},{4,6},{6,4},{5,7},{7,5},{8,10},{10,8},{9,1... | collective-permute-start | bytes 208904 | tf_op jit(solution)/shard_map/ppermute | solution.py:361
  16.8 9.2 %collective-permute-start.11 = (bf16[272,128]{1,0:T(8,128)(2,1)S(1)}, bf16[272,128]{1,0:T(8,128)(2,1)S(1)}, u32[]{:S(2)}, u32[]{:S(2)}) collective-permute-start(bf16[272,128]{1,0:T(8,128)(2,1)S(1)} %get-tuple-element.48), channel_id=1, source_target_pairs={{0,24},{4,28},{8,16},{12,20},{16,8},{20,12},{24,0},{28,4},{1,25},{... | collective-permute-start | bytes 208904 | tf_op jit(solution)/shard_map/ppermute | solution.py:371
  17.3 11.1 %collective-permute-start.12 = (bf16[272,128]{1,0:T(8,128)(2,1)S(1)}, bf16[272,128]{1,0:T(8,128)(2,1)S(1)}, u32[]{:S(2)}, u32[]{:S(2)}) collective-permute-start(bf16[272,128]{1,0:T(8,128)(2,1)S(1)} %get-tuple-element.49), channel_id=1, source_target_pairs={{0,28},{4,24},{8,20},{12,16},{16,12},{20,8},{24,4},{28,0},{1,29},{... | collective-permute-start | bytes 208904 | tf_op jit(solution)/shard_map/ppermute | solution.py:371
  19.7 8.8 %collective-permute-start.8 = (bf16[272,128]{1,0:T(8,128)(2,1)S(1)}, bf16[272,128]{1,0:T(8,128)(2,1)S(1)}, u32[]{:S(2)}, u32[]{:S(2)}) collective-permute-start(bf16[272,128]{1,0:T(8,128)(2,1)S(1)} %get-tuple-element.43), channel_id=1, source_target_pairs={{0,16},{4,20},{8,24},{12,28},{16,0},{20,4},{24,8},{28,12},{1,17},{... | collective-permute-start | bytes 208904 | tf_op jit(solution)/shard_map/ppermute | solution.py:371
  21.1 7.4 %collective-permute-start.9 = (bf16[272,128]{1,0:T(8,128)(2,1)S(1)}, bf16[272,128]{1,0:T(8,128)(2,1)S(1)}, u32[]{:S(2)}, u32[]{:S(2)}) collective-permute-start(bf16[272,128]{1,0:T(8,128)(2,1)S(1)} %get-tuple-element.44), channel_id=1, source_target_pairs={{0,20},{4,16},{8,28},{12,24},{16,4},{20,0},{24,12},{28,8},{1,21},{... | collective-permute-start | bytes 208904 | tf_op jit(solution)/shard_map/ppermute | solution.py:371
  23.3 6.0 %collective-permute-start.3 = (bf16[272,128]{1,0:T(8,128)(2,1)S(1)}, bf16[272,128]{1,0:T(8,128)(2,1)S(1)}, u32[]{:S(2)}, u32[]{:S(2)}) collective-permute-start(bf16[272,128]{1,0:T(8,128)(2,1)S(1)} %get-tuple-element.37), channel_id=1, source_target_pairs={{0,4},{4,0},{8,12},{12,8},{16,20},{20,16},{24,28},{28,24},{1,5},{5... | collective-permute-start | bytes 208904 | tf_op jit(solution)/shard_map/ppermute | solution.py:371
  26.0 4.3 %collective-permute-start.4 = (bf16[272,128]{1,0:T(8,128)(2,1)S(1)}, bf16[272,128]{1,0:T(8,128)(2,1)S(1)}, u32[]{:S(2)}, u32[]{:S(2)}) collective-permute-start(bf16[272,128]{1,0:T(8,128)(2,1)S(1)} %get-tuple-element.38), channel_id=1, source_target_pairs={{0,8},{4,12},{8,0},{12,4},{16,24},{20,28},{24,16},{28,20},{1,9},{5... | collective-permute-start | bytes 208904 | tf_op jit(solution)/shard_map/ppermute | solution.py:371
  28.4 5.2 %collective-permute-start.5 = (bf16[272,128]{1,0:T(8,128)(2,1)S(1)}, bf16[272,128]{1,0:T(8,128)(2,1)S(1)}, u32[]{:S(2)}, u32[]{:S(2)}) collective-permute-start(bf16[272,128]{1,0:T(8,128)(2,1)S(1)} %get-tuple-element.39), channel_id=1, source_target_pairs={{0,12},{4,8},{8,4},{12,0},{16,28},{20,24},{24,20},{28,16},{1,13},{... | collective-permute-start | bytes 208904 | tf_op jit(solution)/shard_map/ppermute | solution.py:371
  35.1 8.0 %collective-permute-start.13 = (f32[4,4,32,128]{3,2,1,0:T(8,128)S(1)}, f32[4,4,32,128]{3,2,1,0:T(8,128)S(1)}, u32[]{:S(2)}, u32[]{:S(2)}) collective-permute-start(f32[4,4,32,128]{3,2,1,0:T(8,128)S(1)} %get-tuple-element.59), channel_id=1, source_target_pairs={{0,1},{1,0},{2,3},{3,2},{4,5},{5,4},{6,7},{7,6},{8,9},{9,8},{10,11... | collective-permute-start | bytes 786440 | tf_op jit(solution)/shard_map/ppermute | solution.py:396
  35.2 6.7 %collective-permute-start.14 = (f32[2,32,128]{2,1,0:T(8,128)S(1)}, f32[2,32,128]{2,1,0:T(8,128)S(1)}, u32[]{:S(2)}, u32[]{:S(2)}) collective-permute-start(f32[2,32,128]{2,1,0:T(8,128)S(1)} %shard_map.51), channel_id=1, source_target_pairs={{1,5},{5,9},{9,13},{13,17},{17,21},{21,25},{25,29},{4,0},{8,4},{12... | collective-permute-start | bytes 98312 | tf_op jit(solution)/shard_map/ppermute | solution.py:390
  41.9 1.2 %collective-permute-start.15 = (f32[2,32,128]{2,1,0:T(8,128)S(1)}, f32[2,32,128]{2,1,0:T(8,128)S(1)}, u32[]{:S(2)}, u32[]{:S(2)}) collective-permute-start(f32[2,32,128]{2,1,0:T(8,128)S(1)} %collective-permute-done.14.mine), channel_id=1, source_target_pairs={{0,1},{1,0},{2,3},{3,2},{4,5},{5,4},{6,7},{7,6},{8,9},{9,8},{10,11... | collective-permute-start | bytes 98312 | tf_op jit(solution)/shard_map/ppermute | solution.py:397
